TPU v7x, 256 devices: a whole 4x4x8 slice. The times are simulated.
256 devices in a mesh: row: 64 (over x, z_lo, y), col: 4 (over z_hi, core).
Axes of the slice: x: 4, y: 4, z: 8 (z_hi: 2, z_lo: 4; z = z_hi * 4 + z_lo), core: 2. Of those that a mesh axis runs over, the one named last changes fastest.
Arguments:
- pair_rep: bfloat16 [1024, 1024, 128], P('row', 'col'), may hold values from -6 to 6
- chain_len: int32 [16], replicated, may hold values from 1 to 64, as said below
- tri_gain: float32 [128], replicated, may hold values from 0.5 to 2
- tri_in: bfloat16 [128, 640], replicated, may hold values from -0.5 to 0.5
- sum_gain: float32 [128], replicated, may hold values from 0.5 to 2
- tri_out: bfloat16 [128, 128], replicated, may hold values from -0.5 to 0.5
- att_gain: float32 [128], replicated, may hold values from 0.5 to 8
- att_in: bfloat16 [128, 512], replicated, may hold values from -0.5 to 0.5
- att_bias: bfloat16 [128, 4], replicated, may hold values from -2 to 2
- att_out: bfloat16 [128, 128], replicated, may hold values from -4 to 4
Outputs:
- new_pair: bfloat16 [1024, 1024, 128], P('row', 'col')
Inputs may be any that keep to these rules, and one draw needn't show every extreme that they name: `chain_len`: one chain in every draw has all 64 slots live.
All inputs are finite; a program needn't handle non-finite values.
Results may differ from a plain program's by a relative error of at most 0.039.
The roundings to bfloat16 on the way count: a program that leaves them out, or rounds other values in their place, can miss the bound.
Values may be sent and summed in bfloat16 or wider, within the bound.
A program may use at most 128 MiB of HBM per device.

v0:
```python
import math

import jax
import jax.numpy as jnp
from jax import lax
from jax.sharding import PartitionSpec as P

CH = 128
H = 4
DH = 32
KCD = 16
SLOT = 64


EPSILON = 1e-05
NEG_SCORE = -1e30


def layer_norm(values, norm_gain):
    values = values.astype(jnp.float32)
    centre = values - jnp.mean(values, axis=-1, keepdims=True)
    spread = jnp.mean(centre * centre, axis=-1, keepdims=True)
    return centre * lax.rsqrt(spread + EPSILON) * norm_gain


def live_tokens(chain_len):
    positions = lax.broadcasted_iota(jnp.int32, (chain_len.shape[0], SLOT), 1)
    return (positions < chain_len[:, None]).astype(jnp.float32).reshape(-1)


def attend_heads(query_pair, kv_all, bias_pair, key_live):

    def attend_row(inputs):
        query_row, kv_row = inputs
        keys_row = kv_row[:, : 2 * DH].reshape(kv_row.shape[0], 2, DH)
        values_row = kv_row[:, 2 * DH :].reshape(kv_row.shape[0], 2, DH)
        scores = (
            jnp.einsum("jhd,khd->hjk", query_row, keys_row, preferred_element_type=jnp.float32)
            / math.sqrt(DH)
            + bias_pair
        )
        scores = jnp.where(key_live[None, None, :], scores, NEG_SCORE)
        row_top = jnp.max(scores, axis=-1, keepdims=True)
        weights = jnp.exp(scores - row_top).astype(jnp.bfloat16)
        totals = jnp.sum(weights, axis=-1, dtype=jnp.float32)
        summed = jnp.einsum("hjk,khd->jhd", weights, values_row, preferred_element_type=jnp.float32)
        return summed / jnp.transpose(totals)[:, :, None]

    return lax.map(attend_row, (query_pair, kv_all))


def body(
    pair_rep, chain_len, tri_gain, tri_in, sum_gain, tri_out, att_gain, att_in, att_bias, att_out
):
    row_count = pair_rep.shape[0]
    col_count = pair_rep.shape[1]
    row_start = lax.axis_index("row") * row_count
    col_start = lax.axis_index("col") * col_count
    live_all = live_tokens(chain_len)
    live_rows = lax.dynamic_slice_in_dim(live_all, row_start, row_count)
    live_cols = lax.dynamic_slice_in_dim(live_all, col_start, col_count)
    tri_norm = layer_norm(pair_rep, tri_gain).astype(jnp.bfloat16)
    out_gate = jax.nn.sigmoid(
        jnp.dot(tri_norm, tri_in[:, 4 * CH :], preferred_element_type=jnp.float32)
    )
    group_proj = jnp.dot(tri_norm[:, :KCD], tri_in[:, : 4 * CH], preferred_element_type=jnp.float32)
    pair_live = live_rows[:, None, None] * live_cols[None, :KCD, None]
    left_edge = (
        jax.nn.sigmoid(group_proj[..., :CH]) * group_proj[..., CH : 2 * CH] * pair_live
    ).astype(jnp.bfloat16)
    right_edge = (
        jax.nn.sigmoid(group_proj[..., 2 * CH : 3 * CH])
        * group_proj[..., 3 * CH : 4 * CH]
        * pair_live
    ).astype(jnp.bfloat16)
    right_all = lax.all_gather(right_edge, "row", axis=0, tiled=True)
    tri_sum = lax.psum_scatter(
        jnp.einsum("ikc,jkc->jic", left_edge, right_all, preferred_element_type=jnp.float32),
        "col",
        scatter_dimension=0,
        tiled=True,
    )
    sum_norm = layer_norm(tri_sum, sum_gain).astype(jnp.bfloat16)
    update = jnp.dot(sum_norm, tri_out, preferred_element_type=jnp.float32)
    mid_pair = (pair_rep.astype(jnp.float32) + out_gate * jnp.transpose(update, (1, 0, 2))).astype(
        jnp.bfloat16
    )
    head_width = H * DH
    att_norm = layer_norm(mid_pair, att_gain).astype(jnp.bfloat16)
    queries = jnp.dot(att_norm, att_in[:, :head_width], preferred_element_type=jnp.float32).astype(
        jnp.bfloat16
    )
    att_gate = jax.nn.sigmoid(
        jnp.dot(att_norm, att_in[:, 3 * head_width :], preferred_element_type=jnp.float32)
    )
    pair_bias = jnp.einsum(
        "rcd,dh->hrc", att_norm, att_bias, preferred_element_type=jnp.float32
    ).astype(jnp.bfloat16)
    bias_rows = lax.all_gather(pair_bias, "row", axis=1, tiled=True)
    bias_local = lax.all_to_all(bias_rows, "col", split_axis=1, concat_axis=2, tiled=True)
    key_live = live_all > 0.5
    pieces = []
    for pair_index in range(H // 2):
        head_low = 2 * pair_index * DH
        head_high = head_low + 2 * DH
        kv_weight = jnp.concatenate(
            [
                att_in[:, head_width + head_low : head_width + head_high],
                att_in[:, 2 * head_width + head_low : 2 * head_width + head_high],
            ],
            axis=1,
        )
        kv_local = jnp.dot(att_norm, kv_weight, preferred_element_type=jnp.float32).astype(
            jnp.bfloat16
        )
        kv_all = lax.all_gather(kv_local, "col", axis=1, tiled=True)
        query_pair = queries[:, :, head_low:head_high].reshape(row_count, col_count, 2, DH)
        bias_pair = bias_local[2 * pair_index : 2 * pair_index + 2]
        pieces.append(attend_heads(query_pair, kv_all, bias_pair, key_live))
    attended = jnp.concatenate(pieces, axis=2).reshape(row_count, col_count, head_width)
    attended = (attended * att_gate).astype(jnp.bfloat16)
    new_pair = (
        mid_pair.astype(jnp.float32)
        + jnp.dot(attended, att_out, preferred_element_type=jnp.float32)
    ).astype(jnp.bfloat16)
    return new_pair


def solution(mesh):
    placed = (P("row", "col", None), P(), P(), P(), P(), P(), P(), P(), P(), P())
    return jax.shard_map(
        body, mesh=mesh, in_specs=placed, out_specs=P("row", "col", None), check_vma=False
    )
```

profile of v0, /device:TPU:25, one launch (start us, length us, event | category | flops | bytes accessed | tf_op | source)
XLA Modules:
  0.0 1171.6 jit_solution(7417267003332203597)
XLA Ops:
  11.5 306.7 %all-gather.5.cloned.1.call-done = bf16[1024,16,128]{2,1,0:T(8,128)(2,1)} async-done(((bf16[16,16,128]{2,1,0:T(8,128)(2,1)}), bf16[1024,16,128]{2,1,0:T(8,128)(2,1)}) %all-gather.5.cloned.1.call-update) | async-done | bytes 4194320 | tf_op jit(solution)/shard_map/all_gather | solution.py:76
  318.2 24.9 %copy.35 = bf16[1024,16,128]{1,0,2:T(8,128)(2,1)} copy(bf16[1024,16,128]{2,1,0:T(8,128)(2,1)} %all-gather.5.cloned.1.call-done) | data formatting | bytes 8388608 | tf_op jit(solution)/shard_map/all_gather | solution.py:76
  343.1 16.8 %convolution_bitcast_fusion.2 = f32[1024,16,128]{0,1,2:T(8,128)} fusion(bf16[1024,16,128]{1,0,2:T(8,128)(2,1)} %copy.35, bf16[16,16,128]{1,0,2:T(8,128)(2,1)S(1)} %copy.36), kind=kOutput, calls=%fused_computation.44 | convolution fusion | flops 67108864 | bytes 12648448 | tf_op jit(solution)/shard_map/ikc,jkc->jic/dot_general | solution.py:78
  359.9 179.7 %reduce-scatter.2.cloned.1.call-done = f32[256,16,128]{0,1,2:T(8,128)} async-done(((f32[1024,16,128]{0,1,2:T(8,128)}), f32[256,16,128]{0,1,2:T(8,128)}) %reduce-scatter.2.cloned.1.call-update) | async-done | bytes 2097168 | tf_op jit(solution)/shard_map/reduce_scatter | solution.py:77
  539.7 1.9 reduce_sum.74
  547.3 292.4 %all-gather.9.cloned.1.call-done = bf16[4,1024,256]{2,0,1:T(4,128)(2,1)} async-done(((bf16[4,16,256]{2,0,1:T(4,128)(2,1)}), bf16[4,1024,256]{2,0,1:T(4,128)(2,1)}) %all-gather.9.cloned.1.call-update) | async-done | bytes 2097168 | tf_op jit(solution)/shard_map/all_gather | solution.py:99
  839.7 66.5 %all-to-all-start = ((bf16[4,1024,256]{2,0,1:T(4,128)(2,1)}), bf16[4,1024,256]{2,0,1:T(4,128)(2,1)S(1)}, u32[]{:S(2)}, u32[]{:S(2)}) async-start(bf16[4,1024,256]{2,0,1:T(4,128)(2,1)} %all-gather.9.cloned.1.call-done), calls=%async_computation.1 | async-start | bytes 4194304 | tf_op jit(solution)/shard_map/all_to_all | solution.py:100
  909.4 43.6 %all-to-all-done = bf16[4,1024,256]{2,0,1:T(4,128)(2,1)S(1)} async-done(((bf16[4,1024,256]{2,0,1:T(4,128)(2,1)}), bf16[4,1024,256]{2,0,1:T(4,128)(2,1)S(1)}, u32[]{:S(2)}, u32[]{:S(2)}) %all-to-all-start) | async-done | bytes 2097184 | tf_op jit(solution)/shard_map/all_to_all | solution.py:100
  953.0 2.3 fusion.96
  956.9 25.1 %all-gather.7.cloned.1.call-done = bf16[16,1024,128]{2,1,0:T(8,128)(2,1)} async-done(((bf16[16,256,128]{2,1,0:T(8,128)(2,1)}), bf16[16,1024,128]{2,1,0:T(8,128)(2,1)}) %all-gather.7.cloned.1.call-update) | async-done | bytes 4194320 | tf_op jit(solution)/shard_map/all_gather | solution.py:116
  983.2 86.3 %while.22 = (s32[]{:T(128)}, f32[16,256,2,32]{1,3,2,0:T(8,128)}, bf16[16,1024,128]{2,1,0:T(8,128)(2,1)}, bf16[16,256,2,32]{1,3,2,0:T(8,128)(2,1)}, bf16[2,256,10...) while((s32[]{:T(128)}, f32[16,256,2,32]{1,3,2,0:T(8,128)}, ...), condition=%wide.region_10.11_spmd.clone, body=%wide.region_7.10_spmd.clone.sunk | while | flops 108025344 | bytes 10510993 | solution.py:49
  991.1 1.7 convert_reduce_fusion.6
  996.5 1.7 convert_reduce_fusion.6
  1001.9 1.7 convert_reduce_fusion.6
  1007.3 1.7 convert_reduce_fusion.6
  1012.7 1.7 convert_reduce_fusion.6
  1018.1 1.7 convert_reduce_fusion.6
  1023.5 1.7 convert_reduce_fusion.6
  1028.9 1.7 convert_reduce_fusion.6
  1034.3 1.7 convert_reduce_fusion.6
  1039.7 1.7 convert_reduce_fusion.6
  1061.2 1.7 convert_reduce_fusion.6
  1066.6 1.7 convert_reduce_fusion.6
  1069.5 2.0 copy.46
  1073.4 86.3 %while.23 = (s32[]{:T(128)}, f32[16,256,2,32]{1,3,2,0:T(8,128)}, bf16[16,1024,128]{2,1,0:T(8,128)(2,1)}, bf16[16,256,2,32]{1,3,2,0:T(8,128)(2,1)}, bf16[2,256,10...) while((s32[]{:T(128)}, f32[16,256,2,32]{1,3,2,0:T(8,128)}, ...), condition=%wide.region_14.15_spmd.clone, body=%wide.region_11.14_spmd.clone.sunk | while | flops 108025344 | bytes 10510993 | solution.py:49
  1092.1 1.7 convert_reduce_fusion.7
  1102.9 1.7 convert_reduce_fusion.7
  1119.1 1.7 convert_reduce_fusion.7
  1124.5 1.7 convert_reduce_fusion.7
  1146.0 1.7 convert_reduce_fusion.7
  1151.4 1.7 convert_reduce_fusion.7
  1159.7 1.9 pad_maximum_fusion
  (345 shorter events, 163.0 us)
Async XLA Ops:
  6.5 535.9 %copy-start = (bf16[128,128]{1,0:T(8,128)(2,1)S(1)}, bf16[128,128]{1,0:T(8,128)(2,1)}, u32[]{:S(2)}) copy-start(bf16[128,128]{1,0:T(8,128)(2,1)} %param.19) | copy-start | bytes 98308
  6.5 311.7 %all-gather.5.cloned.1.call-start = ((), (), s32[]{:S(2)}) async-start(), calls=%async_computation.2 | async-start | bytes 4259840 | tf_op jit(solution)/shard_map/all_gather | solution.py:76
  7.5 2.1 copy-start.9
  9.0 1.0 copy-start.6
  11.1 528.6 %reduce-scatter.2.cloned.1.call-start = ((), (), s32[]{:S(2)}) async-start(), calls=%async_computation.3 | async-start | bytes 10485760 | tf_op jit(solution)/shard_map/reduce_scatter | solution.py:77
  359.9 182.3 %copy-start.11 = (f32[128]{0:T(128)S(1)}, f32[128]{0:T(128)}, u32[]{:S(2)}) copy-start(f32[128]{0:T(128)} %param.18) | copy-start | bytes 1540
  359.9 479.8 %all-gather.9.cloned.1.call-start = ((), (), s32[]{:S(2)}) async-start(), calls=%async_computation.5 | async-start | bytes 2129920 | tf_op jit(solution)/shard_map/all_gather | solution.py:99
  539.7 2.2 copy-start.2
  543.0 1.5 copy-start.10
  543.0 1.5 copy-start.12
  544.1 363.6 %copy-start.3 = (bf16[16,256,128]{1,2,0:T(8,128)(2,1)}, bf16[16,256,128]{1,2,0:T(8,128)(2,1)S(1)}, u32[]{:S(2)}) copy-start(bf16[16,256,128]{1,2,0:T(8,128)(2,1)S(1)} %get-tuple-element.164) | copy-start | bytes 3145732
  544.1 1.5 copy-start.5
  545.6 436.5 %all-gather.7.cloned.1.call-start = ((), (), s32[]{:S(2)}) async-start(), calls=%async_computation.4 | async-start | bytes 5242880 | tf_op jit(solution)/shard_map/all_gather | solution.py:116
  839.7 113.3 %all-to-all-start = ((bf16[4,1024,256]{2,0,1:T(4,128)(2,1)}), bf16[4,1024,256]{2,0,1:T(4,128)(2,1)S(1)}, u32[]{:S(2)}, u32[]{:S(2)}) async-start(bf16[4,1024,256]{2,0,1:T(4,128)(2,1)} %all-gather.9.cloned.1.call-done), calls=%async_computation.1 | async-start | bytes 4194304 | tf_op jit(solution)/shard_map/all_to_all | solution.py:100
  906.2 166.1 %all-gather.11.cloned.1.call-start = ((), (), s32[]{:S(2)}) async-start(), calls=%async_computation.6 | async-start | bytes 5242880 | tf_op jit(solution)/shard_map/all_gather | solution.py:116
  956.2 27.0 %copy-start.7 = (s32[16]{0:T(128)S(1)}, s32[16]{0:T(128)}, u32[]{:S(2)}) copy-start(s32[16]{0:T(128)} %param.15) | copy-start | bytes 196
  1159.7 1.9 copy-start.4
  1161.6 1.7 copy-start.8
  1161.6 3.5 copy-start.1
Sparse Core Ops, SparseCore 0:
  11.2 306.9 all-gather.4
  360.0 179.6 reduce-scatter.1
  545.7 293.9 all-gather.8
  841.5 140.5 all-gather.6
  983.9 61.6 all-gather.10
where the time goes:
time: 1180 us; the launch traced here: 1170 us
  waiting for transfers between devices  848 us (72%)
  matrix products  156 us (13%)
  local copies, waits for them, and re-layouts  77.3 us (7%)
  starting transfers between devices  66.6 us (6%)
  between operations  13.4 us (1%)
    all_gather x1, waiting for transfers between devices, body(): right_all = lax.all_gather(right_edge, 'row', axis=0, tiled=True)  307 us
    all_gather x1, waiting for transfers between devices, body(): bias_rows = lax.all_gather(pair_bias, 'row', axis=1, tiled=True)  292 us
    reduce_scatter x1, waiting for transfers between devices, body(): lax.psum_scatter(jnp.einsum('ikc,jkc->jic', left_edge, right_all, preferr...  180 us
    all_to_all x1, starting transfers between devices, body(): lax.all_to_all(bias_rows, 'col', split_axis=1, concat_axis=2, tiled=True)  66.5 us
    sub x32, matrix products, attend_row(): weights = jnp.exp(scores - row_top).astype(jnp.bfloat16)  53.7 us
    all_to_all x1, waiting for transfers between devices, body(): lax.all_to_all(bias_rows, 'col', split_axis=1, concat_axis=2, tiled=True)  43.6 us
    dot_general x32, matrix products, attend_row(): jnp.einsum('jhd,khd->hjk', query_row, keys_row, preferred_element_type=jn...  39.5 us
    dot_general x32, matrix products, attend_row(): jnp.einsum('hjk,khd->jhd', weights, values_row, preferred_element_type=jn...  37.2 us
  transfers between devices with their start and end apart: 6, of which 5 were waited for; matrix products, arithmetic and copies ran while one was open for 8% of the time, Pallas kernels for 0%

commit v1 on v0

v1 whole, which is shorter than its diff:
```python
import math

import jax
import jax.numpy as jnp
from jax import lax
from jax.experimental import pallas as pl
from jax.experimental.pallas import tpu as pltpu
from jax.sharding import PartitionSpec as P

CH = 128
H = 4
DH = 32
KCD = 16
SLOT = 64
EPSILON = 1e-05
NEG_SCORE = -1e30
MESH = pl.DeviceIdType.MESH
F32 = jnp.float32
BF16 = jnp.bfloat16


def layer_norm(values, norm_gain):
    values = values.astype(F32)
    centre = values - jnp.mean(values, axis=-1, keepdims=True)
    spread = jnp.mean(centre * centre, axis=-1, keepdims=True)
    return centre * lax.rsqrt(spread + EPSILON) * norm_gain


def live_tokens(chain_len):
    positions = lax.broadcasted_iota(jnp.int32, (chain_len.shape[0], SLOT), 1)
    return (positions < chain_len[:, None]).astype(F32).reshape(-1)


def place():
    row = lax.axis_index("row")
    col = lax.axis_index("col")
    return row // 16, (row // 4) % 4, row % 4, col


def device(x, zl, y, col):
    return (x * 16 + zl * 4 + y, col)


class Spread:
    def __init__(self, pay, buf, s1_send, s1_recv, ring_send, ring_recv):
        self.pay, self.buf = pay, buf
        self.s1_send, self.s1_recv = s1_send, s1_recv
        self.ring_send, self.ring_recv = ring_send, ring_recv
        self.x, self.zl, self.y, self.col = place()
        self.sent = []

    def partner(self, i):
        return device(self.col, (self.zl + i) % 4, self.y, self.x)

    def neighbour(self, h, axis, d):
        along_y = (h == 0) == (axis == 0)
        if along_y:
            return device(self.x, self.zl, (self.y + d + 4) % 4, self.col)
        return device((self.x + d + 4) % 4, self.zl, self.y, self.col)

    def greet(self, barrier):
        def hello(to):
            pl.semaphore_signal(barrier, inc=1, device_id=to, device_id_type=MESH)

        for i in range(1, 4):
            hello(self.partner(i))
        for axis in range(2):
            for d in (1, -1):
                hello(self.neighbour(0, axis, d))

        @pl.when(self.x != self.col)
        def _():
            hello(self.partner(0))

        return 7 + (self.x != self.col).astype(jnp.int32)

    def first(self, i):
        return pltpu.make_async_remote_copy(
            src_ref=self.pay,
            dst_ref=self.buf.at[:, self.col, self.y, self.zl],
            send_sem=self.s1_send.at[i],
            recv_sem=self.s1_recv.at[i],
            device_id=self.partner(i),
            device_id_type=MESH,
        )

    def first_local(self):
        return pltpu.make_async_copy(
            self.pay, self.buf.at[:, self.col, self.y, self.zl], self.s1_send.at[0]
        )

    def first_arrival(self, i):
        return pltpu.make_async_remote_copy(
            src_ref=self.pay,
            dst_ref=self.buf.at[:, self.x, self.y, (self.zl + 4 - i) % 4],
            send_sem=self.s1_send.at[i],
            recv_sem=self.s1_recv.at[i],
            device_id=self.partner(i),
            device_id_type=MESH,
        )

    def start(self):
        @pl.when(self.x != self.col)
        def _():
            self.first(0).start()

        @pl.when(self.x == self.col)
        def _():
            self.first_local().start()

        for i in range(1, 4):
            self.first(i).start()

    def landed(self):
        @pl.when(self.x != self.col)
        def _():
            self.first_arrival(0).wait_recv()
            self.first(0).wait_send()

        @pl.when(self.x == self.col)
        def _():
            self.first_local().wait()

        for i in range(1, 4):
            self.first_arrival(i).wait_recv()

    def piece(self, h, f, s, sub):
        xi, yi = (s, f) if h == 0 else (f, s)
        return self.buf.at[h, (self.x + xi) % 4, (self.y + yi) % 4, pl.ds(2 * sub, 2)]

    def slot(self, h, f, s, sub):
        return ((h * 4 + f) * 4 + s) * 2 + sub

    def send(self, h, f, s, sub, axis, d):
        there = ((f - d) % 4, s) if axis == 0 else (f, (s - d) % 4)
        copy = pltpu.make_async_remote_copy(
            src_ref=self.piece(h, f, s, sub),
            dst_ref=self.piece(h, f, s, sub),
            send_sem=self.ring_send.at[len(self.sent)],
            recv_sem=self.ring_recv.at[self.slot(h, *there, sub)],
            device_id=self.neighbour(h, axis, d),
            device_id_type=MESH,
        )
        copy.start()
        self.sent.append(copy)

    def own(self):
        for axis in range(2):
            for step in range(2):
                for h in range(2):
                    self.send(h, 0, 0, step, axis, 1)
                    self.send(h, 0, 0, 1 - step, axis, -1)

    def arrive(self, h, f, s, sub):
        pltpu.make_async_remote_copy(
            src_ref=self.piece(h, f, s, sub),
            dst_ref=self.piece(h, f, s, sub),
            send_sem=self.ring_send.at[0],
            recv_sem=self.ring_recv.at[self.slot(h, f, s, sub)],
            device_id=self.neighbour(h, 0, 1),
            device_id_type=MESH,
        ).wait_recv()

    def take(self, h, f, s, sub):
        self.arrive(h, f, s, sub)
        if s == 0:
            if f == 3 and sub == 0:
                self.send(h, f, s, sub, 0, 1)
            if f == 1 and sub == 1:
                self.send(h, f, s, sub, 0, -1)
            self.send(h, f, s, sub, 1, 1 if sub == 0 else -1)
            self.send(h, f, s, sub, 1, -1 if sub == 0 else 1)
        else:
            if s == 3 and sub == 0:
                self.send(h, f, s, sub, 1, 1)
            if s == 1 and sub == 1:
                self.send(h, f, s, sub, 1, -1)

    def order(self):
        near = [(3, 0), (1, 1), (3, 1), (1, 0)]
        steps = [(a, 0, sub) for a, sub in near]
        steps += [(0, a, sub) for a, sub in near]
        steps += [(2, 0, 0), (2, 0, 1)]
        for f in (3, 1):
            steps += [(f, a, sub) for a, sub in near]
        steps += [(0, 2, 0), (0, 2, 1)]
        steps += [(2, a, sub) for a, sub in near]
        steps += [(f, 2, sub) for f in (3, 1, 2) for sub in range(2)]
        return [(h, *step) for step in steps for h in range(2)]

    def finish(self):
        for i in range(1, 4):
            self.first(i).wait_send()
        for copy in self.sent:
            copy.wait_send()


SPREAD_SEMS = [
    pltpu.SemaphoreType.DMA((4,)),
    pltpu.SemaphoreType.DMA((4,)),
    pltpu.SemaphoreType.DMA((60,)),
    pltpu.SemaphoreType.DMA((64,)),
]


def edge_exchange(right, left, right_all, left_all, s1s, s1r, rs, rr, l_send, l_recv, l_own):
    spread = Spread(right, right_all, s1s, s1r, rs, rr)
    x, zl, y, col = spread.x, spread.zl, spread.y, spread.col
    barrier = pltpu.get_barrier_semaphore()
    count = spread.greet(barrier)
    peers = [device(x, zl, y, col ^ 1), device(x, zl, y, col ^ 2), device(x, zl, y, col ^ 3)]
    for peer in peers:
        pl.semaphore_signal(barrier, inc=1, device_id=peer, device_id_type=MESH)
    pl.semaphore_wait(barrier, count + 3)
    spread.start()

    def left_copy(j, block):
        return pltpu.make_async_remote_copy(
            src_ref=left,
            dst_ref=left_all.at[block],
            send_sem=l_send.at[j],
            recv_sem=l_recv.at[j],
            device_id=peers[j],
            device_id_type=MESH,
        )

    for j in range(3):
        left_copy(j, col).start()
    own = pltpu.make_async_copy(left, left_all.at[col], l_own.at[0])
    own.start()
    spread.landed()
    spread.own()
    for step in spread.order():
        spread.take(*step)
    own.wait()
    for j in range(3):
        left_copy(j, col).wait_send()
        left_copy(j, col ^ (j + 1)).wait_recv()
    spread.finish()


def norm_exchange(bias, norm, bias_all, norm_all, held, s1s, s1r, rs, rr, sib, hop1s, hop1r, hop2s, hop2r, fwds, fwdr):
    spread = Spread(bias, bias_all, s1s, s1r, rs, rr)
    x, zl, y, col = spread.x, spread.zl, spread.y, spread.col
    core = col % 2
    z = (col // 2) * 4 + zl

    def at_z(offset):
        there = (z + offset + 8) % 8
        return device(x, there % 4, y, (there // 4) * 2 + core)

    def col_at(offset):
        return (((z + offset + 8) % 8) // 4) * 2 + core

    sibling = device(x, zl, y, col ^ 1)
    barrier = pltpu.get_barrier_semaphore()
    count = spread.greet(barrier)
    for peer in (sibling, at_z(2), at_z(-2)):
        pl.semaphore_signal(barrier, inc=1, device_id=peer, device_id_type=MESH)
    pl.semaphore_wait(barrier, count + 3)

    def remote(src, dst, send, recv, to):
        return pltpu.make_async_remote_copy(
            src_ref=src, dst_ref=dst, send_sem=send, recv_sem=recv, device_id=to, device_id_type=MESH
        )

    def rows(way, c):
        return pl.ds(8 * way + 2 * c, 2)

    def step(way):
        return 2 if way == 0 else -2

    def hop1(way, c):
        return remote(
            norm.at[rows(way, c)], held.at[way, c], hop1s.at[way, c], hop1r.at[way, c], at_z(step(way))
        )

    def hop2(way, c):
        return remote(
            held.at[way, c],
            norm_all.at[col_at(-step(way)), rows(way, c)],
            hop2s.at[way, c],
            hop2r.at[way, c],
            at_z(step(way)),
        )

    def hop2_arrival(way, c):
        return remote(
            held.at[way, c],
            norm_all.at[col ^ 2, rows(way, c)],
            hop2s.at[way, c],
            hop2r.at[way, c],
            at_z(step(way)),
        )

    def forward(way, c, block):
        return remote(
            norm_all.at[col ^ 2, rows(way, c)],
            norm_all.at[block, rows(way, c)],
            fwds.at[way, c],
            fwdr.at[way, c],
            sibling,
        )

    spread.start()
    for c in range(4):
        for way in range(2):
            hop1(way, c).start()
    own = pltpu.make_async_copy(norm, norm_all.at[col], sib.at[0])
    own.start()
    to_sibling = remote(norm, norm_all.at[col], sib.at[1], sib.at[2], sibling)
    to_sibling.start()
    spread.landed()
    spread.own()

    def relay(way, c):
        hop1(way, c).wait_recv()
        hop2(way, c).start()

    def last(way, c):
        hop2_arrival(way, c).wait_recv()
        forward(way, c, col ^ 2).start()

    extra = []
    for c in range(5):
        for way in range(2):
            if c < 4:
                extra.append((relay, way, c))
        for way in range(2):
            if c > 0:
                extra.append((last, way, c - 1))
    order = spread.order()
    for at, each in enumerate(order):
        spread.take(*each)
        if at % 4 == 3 and extra:
            fn, way, c = extra.pop(0)
            fn(way, c)
    for fn, way, c in extra:
        fn(way, c)
    own.wait()
    to_sibling.wait_send()
    remote(norm, norm_all.at[col ^ 1], sib.at[1], sib.at[2], sibling).wait_recv()
    for c in range(4):
        for way in range(2):
            hop1(way, c).wait_send()
            hop2(way, c).wait_send()
            forward(way, c, col ^ 2).wait_send()
            forward(way, c, col ^ 3).wait_recv()
    spread.finish()


ANY = pl.BlockSpec(memory_space=pl.ANY)


def exchange_edges(right, left):
    return pl.pallas_call(
        edge_exchange,
        name="edge_exchange",
        out_shape=(
            jax.ShapeDtypeStruct((2, 4, 4, 4) + right.shape[1:], right.dtype),
            jax.ShapeDtypeStruct((4,) + left.shape, left.dtype),
        ),
        in_specs=[ANY, ANY],
        out_specs=(ANY, ANY),
        scratch_shapes=SPREAD_SEMS
        + [
            pltpu.SemaphoreType.DMA((3,)),
            pltpu.SemaphoreType.DMA((3,)),
            pltpu.SemaphoreType.DMA((1,)),
        ],
        compiler_params=pltpu.CompilerParams(collective_id=0, has_side_effects=True),
    )(right, left)


def exchange_norms(bias, norm):
    return pl.pallas_call(
        norm_exchange,
        name="norm_exchange",
        out_shape=(
            jax.ShapeDtypeStruct((2, 4, 4, 4) + bias.shape[1:], bias.dtype),
            jax.ShapeDtypeStruct((4,) + norm.shape, norm.dtype),
        ),
        in_specs=[ANY, ANY],
        out_specs=(ANY, ANY),
        scratch_shapes=[pltpu.VMEM((2, 4, 2) + norm.shape[1:], norm.dtype)]
        + SPREAD_SEMS
        + [pltpu.SemaphoreType.DMA((3,))]
        + [pltpu.SemaphoreType.DMA((2, 4))] * 6,
        compiler_params=pltpu.CompilerParams(collective_id=1, has_side_effects=True),
    )(bias, norm)


def triangle_kernel(
    right, left, pair, tri_gain, tri_in, sum_gain, tri_out, att_gain, att_bias,
    mid, norm, bias, left_wide, normed, bias_wide,
):
    at = pl.program_id(0)

    @pl.when(at == 0)
    def _():
        for b in range(4):
            left_wide[pl.ds(16 * b, 16)] = left[b].astype(F32)

    def contract(q, sums):
        block, half = q // 2, q % 2
        sums = list(sums)
        for k in range(8):
            edge = right[half, block, 0, 0, k].astype(F32)
            token = block * 16 + half * 8 + k
            for i in range(16):
                sums[i] = sums[i] + edge * left_wide[token, pl.ds(i, 1), :]
        return tuple(sums)

    zero = jnp.zeros((16, CH), F32)
    sums = lax.fori_loop(0, 8, contract, (zero,) * 16)
    for i in range(16):
        normed[i] = layer_norm(sums[i], sum_gain[...]).astype(BF16)
    update = jnp.dot(normed[...].reshape(256, CH), tri_out[...], preferred_element_type=F32)
    tile = pair[...].reshape(256, CH).astype(F32)
    tri_norm = layer_norm(tile, tri_gain[...]).astype(BF16)
    gate = jax.nn.sigmoid(jnp.dot(tri_norm, tri_in[...], preferred_element_type=F32))
    mid_tile = (tile + gate * update).astype(BF16)
    mid[...] = mid_tile.reshape(16, 16, CH)
    att = layer_norm(mid_tile, att_gain[...]).astype(BF16)
    norm[:, pl.ds(pl.multiple_of(at * 16, 16), 16), :] = att.reshape(16, 16, CH)

    @pl.when(at == 15)
    def _():
        for i in range(16):
            rows = lax.dot_general(
                att_bias[...], norm[i], (((1,), (1,)), ((), ())), preferred_element_type=F32
            )
            for h in range(H):
                bias_wide[h, pl.ds(i, 1), :] = rows[h : h + 1]
        for h in range(H):
            bias[h // 2, h % 2] = bias_wide[h].astype(BF16)


def triangle(right_all, left_all, pair_rep, tri_gain, tri_in, sum_gain, tri_out, att_gain, att_bias):
    whole = lambda *shape: pl.BlockSpec(shape, lambda t: (0,) * len(shape))
    bias_rows = jnp.zeros((8, CH), BF16).at[:H].set(att_bias.T)
    return pl.pallas_call(
        triangle_kernel,
        name="triangle",
        grid=(16,),
        out_shape=(
            jax.ShapeDtypeStruct((16, 256, CH), BF16),
            jax.ShapeDtypeStruct((16, 256, CH), BF16),
            jax.ShapeDtypeStruct((2, 2, 16, 256), BF16),
        ),
        in_specs=[
            pl.BlockSpec((2, 4, 1, 1, 8, 16, CH), lambda t: (0, 0, t % 4, t // 4, 0, 0, 0)),
            whole(4, 16, 16, CH),
            pl.BlockSpec((16, 16, CH), lambda t: (0, t, 0)),
            whole(1, CH),
            pl.BlockSpec((CH, CH), lambda t: (0, 4)),
            whole(1, CH),
            whole(CH, CH),
            whole(1, CH),
            whole(8, CH),
        ],
        out_specs=(
            pl.BlockSpec((16, 16, CH), lambda t: (0, t, 0)),
            whole(16, 256, CH),
            whole(2, 2, 16, 256),
        ),
        scratch_shapes=[
            pltpu.VMEM((64, 16, CH), F32),
            pltpu.VMEM((16, 16, CH), BF16),
            pltpu.VMEM((H, 16, 256), F32),
        ],
        compiler_params=pltpu.CompilerParams(vmem_limit_bytes=32 << 20),
    )(
        right_all, left_all, pair_rep, tri_gain.reshape(1, CH), tri_in, sum_gain.reshape(1, CH),
        tri_out, att_gain.reshape(1, CH), bias_rows,
    )


TILE = 128


def attention_kernel(own, norm, mid, bias, dead, att_in, att_out, new, bias_wide):
    row = pl.program_id(0)

    @pl.when(row == 0)
    def _():
        for h in range(H):
            for block in range(4):
                masked = dead[:, pl.ds(256 * block, 256)]
                for part in range(16):
                    some = bias[h // 2, block, part % 4, part // 4, h % 2].astype(F32)
                    bias_wide[h, pl.ds(16 * part, 16), pl.ds(256 * block, 256)] = some + masked

    here = norm[...].reshape(4 * 256, CH)
    kv = jnp.dot(here, att_in[:, CH : 3 * CH], preferred_element_type=F32).astype(BF16)
    keys = kv[:, :CH]
    values = jnp.concatenate([kv[:, CH:], jnp.ones((1024, CH), BF16)], axis=1)
    mine = own[0]
    queries = jnp.dot(mine, att_in[:, :CH], preferred_element_type=F32).astype(BF16)
    gate = jax.nn.sigmoid(jnp.dot(mine, att_in[:, 3 * CH :], preferred_element_type=F32))
    lane_head = lax.broadcasted_iota(jnp.int32, (TILE, CH), 1) // DH
    for t in range(256 // TILE):
        rows = slice(t * TILE, (t + 1) * TILE)
        attended = jnp.zeros((TILE, CH), F32)
        for h in range(H):
            query = jnp.where(lane_head == h, queries[rows], jnp.zeros((), BF16))
            scores = lax.dot_general(
                query, keys, (((1,), (1,)), ((), ())), preferred_element_type=F32
            )
            scores = scores * (1.0 / math.sqrt(DH)) + bias_wide[h, pl.ds(t * TILE, TILE), :]
            top = jnp.max(scores, axis=-1, keepdims=True)
            weights = jnp.exp(scores - top).astype(BF16)
            summed = jnp.dot(weights, values, preferred_element_type=F32)
            attended = jnp.where(lane_head == h, summed[:, :CH] / summed[:, CH:], attended)
        attended = (attended * gate[rows]).astype(BF16)
        add = jnp.dot(attended, att_out[...], preferred_element_type=F32)
        new[0, pl.ds(t * TILE, TILE), :] = (mid[0, pl.ds(t * TILE, TILE), :].astype(F32) + add).astype(BF16)


def attention(own, norm_all, mid, bias_all, dead, att_in, att_out):
    whole = lambda *shape: pl.BlockSpec(shape, lambda t: (0,) * len(shape))
    one_row = pl.BlockSpec((1, 256, CH), lambda t: (t, 0, 0))
    return pl.pallas_call(
        attention_kernel,
        name="attention",
        grid=(16,),
        out_shape=jax.ShapeDtypeStruct((16, 256, CH), BF16),
        in_specs=[
            one_row,
            pl.BlockSpec((4, 1, 256, CH), lambda t: (0, t, 0, 0)),
            one_row,
            whole(2, 4, 4, 4, 2, 16, 256),
            whole(1, 1024),
            whole(CH, 4 * CH),
            whole(CH, CH),
        ],
        out_specs=one_row,
        scratch_shapes=[pltpu.VMEM((H, 256, 1024), F32)],
        compiler_params=pltpu.CompilerParams(vmem_limit_bytes=48 << 20),
    )(own, norm_all, mid, bias_all, dead, att_in, att_out)


def body(
    pair_rep, chain_len, tri_gain, tri_in, sum_gain, tri_out, att_gain, att_in, att_bias, att_out
):
    row_count = pair_rep.shape[0]
    col_count = pair_rep.shape[1]
    live_all = live_tokens(chain_len)
    live_rows = lax.dynamic_slice_in_dim(live_all, lax.axis_index("row") * row_count, row_count)
    live_cols = lax.dynamic_slice_in_dim(live_all, lax.axis_index("col") * col_count, KCD)
    group_norm = layer_norm(pair_rep[:, :KCD], tri_gain).astype(BF16)
    group_proj = jnp.dot(group_norm, tri_in[:, : 4 * CH], preferred_element_type=F32)
    pair_live = live_rows[:, None, None] * live_cols[None, :, None]
    left_edge = (jax.nn.sigmoid(group_proj[..., :CH]) * group_proj[..., CH : 2 * CH] * pair_live).astype(BF16)
    right_edge = (
        jax.nn.sigmoid(group_proj[..., 2 * CH : 3 * CH]) * group_proj[..., 3 * CH :] * pair_live
    ).astype(BF16)
    left_edge = jnp.transpose(left_edge, (1, 0, 2))
    right_edge = jnp.transpose(right_edge, (1, 0, 2)).reshape(2, 8, 16, CH)
    right_all, left_all = exchange_edges(right_edge, left_edge)
    mid, norm, bias = triangle(
        right_all, left_all, pair_rep, tri_gain, tri_in, sum_gain, tri_out, att_gain, att_bias
    )
    bias_all, norm_all = exchange_norms(bias, norm)
    dead = jnp.where(live_all > 0.5, 0.0, NEG_SCORE).reshape(1, -1)
    return attention(norm, norm_all, mid, bias_all, dead, att_in, att_out)


def solution(mesh):
    placed = (P("row", "col", None), P(), P(), P(), P(), P(), P(), P(), P(), P())
    return jax.shard_map(
        body, mesh=mesh, in_specs=placed, out_specs=P("row", "col", None), check_vma=False
    )
```

time: 1180 us -> 206 us (0.17)
  waiting for transfers between devices: 848 us -> 0 us
  Pallas kernels: 0 us -> 183 us
  matrix products: 156 us -> 1.14 us
  starting transfers between devices: 66.6 us -> 0 us
  local copies, waits for them, and re-layouts: 77.3 us -> 13.3 us
  between operations: 13.4 us -> 0.14 us
    all_gather x4 -> x0, waiting for transfers between devices: 624 us -> none  [the longest x1 307 us: body(): right_all = lax.all_gather(right_edge, 'row', axis=0, tiled=True)]
    pallas_call x0 -> x4, Pallas kernels: none -> 183 us  [the longest x1 63.7 us: exchange_norms(): pl.pallas_call(norm_exchange, name='norm_exchange', out_shape=(jax.ShapeD...]
    reduce_scatter x1 -> x0, waiting for transfers between devices: 180 us -> none  [body(): lax.psum_scatter(jnp.einsum('ikc,jkc->jic', left_edge, right_all, preferr...]
    dot_general x74 -> x1, matrix products: 102 us -> 1.14 us  [body(): jnp.dot(group_norm, tri_in[:, :4 * CH], preferred_element_type=F32)]
    all_to_all x1 -> x0, starting transfers between devices: 66.5 us -> none  [body(): lax.all_to_all(bias_rows, 'col', split_axis=1, concat_axis=2, tiled=True)]
    sub x32 -> x0, matrix products: 53.7 us -> none  [attend_row(): weights = jnp.exp(scores - row_top).astype(jnp.bfloat16)]
    all_to_all x1 -> x0, waiting for transfers between devices: 43.6 us -> none  [body(): lax.all_to_all(bias_rows, 'col', split_axis=1, concat_axis=2, tiled=True)]
    dynamic_slice x66 -> x1, local copies, waits for them, and re-layouts: 35.7 us -> 0.08 us  [body(): lax.dynamic_slice_in_dim(live_all, lax.axis_index('row') * row_count, row...]
  transfers between devices with their start and end apart: 6 -> 0, of which waited for: 5 -> 0; matrix products, arithmetic and copies ran while one was open for 8% -> 0% of each run, Pallas kernels for 0% -> 0%
where the time goes in v1:
time: 206 us; the launch traced here: 203 us
  Pallas kernels  183 us (89%)
  local copies, waits for them, and re-layouts  13.3 us (6%)
  other arithmetic  5.25 us (3%)
    pallas_call x1, Pallas kernels, exchange_norms(): pl.pallas_call(norm_exchange, name='norm_exchange', out_shape=(jax.ShapeD...  63.7 us
    pallas_call x1, Pallas kernels, exchange_edges(): pl.pallas_call(edge_exchange, name='edge_exchange', out_shape=(jax.ShapeD...  50.1 us
    pallas_call x1, Pallas kernels, attention(): pl.pallas_call(attention_kernel, name='attention', grid=(16,), out_shape=...  47.9 us
    pallas_call x1, Pallas kernels, triangle(): pl.pallas_call(triangle_kernel, name='triangle', grid=(16,), out_shape=(j...  21.6 us
    unnamed x28, local copies, waits for them, and re-layouts  12.4 us

profile of v1, /device:TPU:25, one launch (start us, length us, event | category | flops | bytes accessed | tf_op | source)
XLA Modules:
  0.0 203.1 jit_solution(12236605060875798932)
XLA Ops:
  0.0 0.7 scatter.4.att_bias
  0.7 0.7 compare_select_fusion
  1.4 0.1 select_n.23.dead
  1.5 0.7 fusion.20
  2.2 0.1 reshape.128
  2.3 0.1 fusion.21
  2.4 0.1 broadcast_multiply_fusion
  2.4 0.9 convert_reduce_fusion
  3.4 1.0 fusion.2
  4.5 1.0 fusion.4
  5.5 0.0 copy-start.7
  5.5 0.0 copy-start.9
  5.5 1.1 fusion.15
  6.6 0.7 fusion.19
  7.4 50.1 %edge_exchange.1 = (bf16[2,4,4,4,8,16,128]{6,5,4,3,2,1,0:T(8,128)(2,1)}, bf16[4,16,16,128]{3,2,1,0:T(8,128)(2,1)}) custom-call(bf16[2,8,16,128]{3,2,1,0:T(8,128)(2,1)} %bitcast.15, bf16[16,16,128]{2,1,0:T(8,128)(2,1)} %get-tuple-element.31.left), custom_call_target="tpu_custom_call" | custom-call | tf_op jit(solution)/shard_map/edge_exchange/pallas_call | solution.py:356
  57.5 2.2 %copy-done.2 = bf16[2,4,4,4,8,16,128]{6,5,4,3,2,1,0:T(8,128)(2,1)S(1)} copy-done((bf16[2,4,4,4,8,16,128]{6,5,4,3,2,1,0:T(8,128)(2,1)S(1)}, bf16[2,4,4,4,8,16,128]{6,5,4,3,2,1,0:T(8,128)(2,1)}, u32[]{:S(2)}) %copy-start.2) | copy-done | bytes 4194328
  59.7 1.2 copy-done.4
  60.9 0.9 copy-done.5
  61.8 0.9 copy-done.6
  62.8 0.8 copy-done.8
  63.5 0.7 copy-done.11
  64.2 0.7 copy-done.12
  64.8 0.7 copy-done.13
  65.5 21.6 %triangle.1 = (bf16[16,256,128]{2,1,0:T(8,128)(2,1)S(1)}, bf16[16,256,128]{2,1,0:T(8,128)(2,1)S(1)}, bf16[2,2,16,256]{3,2,1,0:T(8,128)(2,1)S(1)}) custom-call(bf16[2,4,4,4,8,16,128]{6,5,4,3,2,1,0:T(8,128)(2,1)S(1)} %copy-done.2, bf16[4,16,16,128]{3,2,1,0:T(8,128)(2,1)S(1)} %copy-done.6, bf16[16,256,128]{2,1,0:T(8,128)(2,1)S(1)} %copy-done.4, ...), custom_call_target="tpu_custom_call" | custom-call | tf_op jit(solution)/shard_map/triangle/pallas_call | solution.py:442
  87.1 0.0 copy-start
  87.1 1.0 copy-done
  88.0 0.6 copy-done.10
  88.6 63.7 %norm_exchange.1 = (bf16[2,4,4,4,2,16,256]{6,5,4,3,2,1,0:T(8,128)(2,1)}, bf16[4,16,256,128]{3,2,1,0:T(8,128)(2,1)}) custom-call(bf16[2,2,16,256]{3,2,1,0:T(8,128)(2,1)} %copy-done.10, bf16[16,256,128]{2,1,0:T(8,128)(2,1)} %copy-done), custom_call_target="tpu_custom_call" | custom-call | tf_op jit(solution)/shard_map/norm_exchange/pallas_call | solution.py:376
  152.3 0.0 copy-start.1
  152.4 1.2 copy-done.1
  153.6 1.6 copy-done.3
  155.2 47.9 %attention.1 = bf16[16,256,128]{2,1,0:T(8,128)(2,1)} custom-call(bf16[16,256,128]{2,1,0:T(8,128)(2,1)S(1)} %copy-done.1, bf16[4,16,256,128]{3,2,1,0:T(8,128)(2,1)} %get-tuple-element.28.norm, bf16[16,256,128]{2,1,0:T(8,128)(2,1)S(1)} %get-tuple-element.29.mid, bf16[2,4,4,4,2,16,256]{6,5,4,3,2,1,0:T(8,128)(2,1)S(1)} %copy-done.3, ...), custom_call_target="tpu_custom_call" | custom-call | tf_op jit(solution)/shard_map/attention/pallas_call | solution.py:523
  (14 shorter events, 0.0 us)
Async XLA Ops:
  5.5 146.9 %copy-start.7 = (bf16[128,512]{1,0:T(8,128)(2,1)S(1)}, bf16[128,512]{1,0:T(8,128)(2,1)}, u32[]{:S(2)}) copy-start(bf16[128,512]{1,0:T(8,128)(2,1)} %att_in.1) | copy-start | bytes 393220
  5.5 146.9 %copy-start.9 = (bf16[128,128]{1,0:T(8,128)(2,1)S(1)}, bf16[128,128]{1,0:T(8,128)(2,1)}, u32[]{:S(2)}) copy-start(bf16[128,128]{1,0:T(8,128)(2,1)} %att_out.1) | copy-start | bytes 98308
  57.5 2.2 %copy-start.2 = (bf16[2,4,4,4,8,16,128]{6,5,4,3,2,1,0:T(8,128)(2,1)S(1)}, bf16[2,4,4,4,8,16,128]{6,5,4,3,2,1,0:T(8,128)(2,1)}, u32[]{:S(2)}) copy-start(bf16[2,4,4,4,8,16,128]{6,5,4,3,2,1,0:T(8,128)(2,1)} %get-tuple-element.24.right) | copy-start | bytes 12582916
  59.7 1.2 copy-start.4
  60.9 0.9 copy-start.5
  61.8 0.9 copy-start.6
  62.8 0.8 copy-start.8
  63.5 0.7 copy-start.11
  64.2 0.7 copy-start.12
  64.8 0.7 copy-start.13
  87.1 1.0 copy-start
  88.0 0.6 copy-start.10
  152.3 1.2 copy-start.1
  153.6 1.6 copy-start.3

commit v2 on v1

--- a/solution.py
+++ b/solution.py
@@ -47,10 +47,14 @@
         self.s1_send, self.s1_recv = s1_send, s1_recv
         self.ring_send, self.ring_recv = ring_send, ring_recv
         self.x, self.zl, self.y, self.col = place()
+        self.swapped = self.x != self.col
         self.sent = []
 
-    def partner(self, i):
-        return device(self.col, (self.zl + i) % 4, self.y, self.x)
+    def partner(self):
+        return device(self.col, self.zl, self.y, self.x)
+
+    def line(self, i):
+        return device(self.x, (self.zl + i) % 4, self.y, self.col)
 
     def neighbour(self, h, axis, d):
         along_y = (h == 0) == (axis == 0)
@@ -63,66 +67,67 @@
             pl.semaphore_signal(barrier, inc=1, device_id=to, device_id_type=MESH)
 
         for i in range(1, 4):
-            hello(self.partner(i))
+            hello(self.line(i))
         for axis in range(2):
             for d in (1, -1):
                 hello(self.neighbour(0, axis, d))
 
-        @pl.when(self.x != self.col)
+        @pl.when(self.swapped)
         def _():
-            hello(self.partner(0))
-
-        return 7 + (self.x != self.col).astype(jnp.int32)
-
-    def first(self, i):
+            hello(self.partner())
+
+        return 7 + self.swapped.astype(jnp.int32)
+
+    def swap(self, arrival):
+        into = (self.x, self.zl) if arrival else (self.col, self.zl)
         return pltpu.make_async_remote_copy(
             src_ref=self.pay,
-            dst_ref=self.buf.at[:, self.col, self.y, self.zl],
+            dst_ref=self.buf.at[:, into[0], self.y, into[1]],
+            send_sem=self.s1_send.at[0],
+            recv_sem=self.s1_recv.at[0],
+            device_id=self.partner(),
+            device_id_type=MESH,
+        )
+
+    def keep(self):
+        return pltpu.make_async_copy(
+            self.pay, self.buf.at[:, self.x, self.y, self.zl], self.s1_send.at[0]
+        )
+
+    def share(self, i, arrival):
+        block = self.buf.at[:, self.x, self.y, (self.zl + 4 - i) % 4 if arrival else self.zl]
+        return pltpu.make_async_remote_copy(
+            src_ref=block,
+            dst_ref=block,
             send_sem=self.s1_send.at[i],
             recv_sem=self.s1_recv.at[i],
-            device_id=self.partner(i),
+            device_id=self.line(i),
             device_id_type=MESH,
         )
 
-    def first_local(self):
-        return pltpu.make_async_copy(
-            self.pay, self.buf.at[:, self.col, self.y, self.zl], self.s1_send.at[0]
-        )
-
-    def first_arrival(self, i):
-        return pltpu.make_async_remote_copy(
-            src_ref=self.pay,
-            dst_ref=self.buf.at[:, self.x, self.y, (self.zl + 4 - i) % 4],
-            send_sem=self.s1_send.at[i],
-            recv_sem=self.s1_recv.at[i],
-            device_id=self.partner(i),
-            device_id_type=MESH,
-        )
-
     def start(self):
-        @pl.when(self.x != self.col)
+        @pl.when(self.swapped)
         def _():
-            self.first(0).start()
-
-        @pl.when(self.x == self.col)
+            self.swap(False).start()
+
+        @pl.when(jnp.logical_not(self.swapped))
         def _():
-            self.first_local().start()
-
-        for i in range(1, 4):
-            self.first(i).start()
+            self.keep().start()
 
     def landed(self):
-        @pl.when(self.x != self.col)
+        @pl.when(self.swapped)
         def _():
-            self.first_arrival(0).wait_recv()
-            self.first(0).wait_send()
-
-        @pl.when(self.x == self.col)
+            self.swap(True).wait_recv()
+            self.swap(False).wait_send()
+
+        @pl.when(jnp.logical_not(self.swapped))
         def _():
-            self.first_local().wait()
-
-        for i in range(1, 4):
-            self.first_arrival(i).wait_recv()
+            self.keep().wait()
+
+        for i in (1, 3, 2):
+            self.share(i, False).start()
+        for i in (1, 3, 2):
+            self.share(i, True).wait_recv()
 
     def piece(self, h, f, s, sub):
         xi, yi = (s, f) if h == 0 else (f, s)
@@ -190,7 +195,7 @@
 
     def finish(self):
         for i in range(1, 4):
-            self.first(i).wait_send()
+            self.share(i, False).wait_send()
         for copy in self.sent:
             copy.wait_send()
 
@@ -239,113 +244,102 @@
     spread.finish()
 
 
-def norm_exchange(bias, norm, bias_all, norm_all, held, s1s, s1r, rs, rr, sib, hop1s, hop1r, hop2s, hop2r, fwds, fwdr):
+def remote(src, dst, send, recv, to):
+    return pltpu.make_async_remote_copy(
+        src_ref=src, dst_ref=dst, send_sem=send, recv_sem=recv, device_id=to, device_id_type=MESH
+    )
+
+
+AHEAD = 8
+
+
+def finish_kernel(
+    bias, norm, mid, dead, att_in, att_out, new,
+    bias_all, norm_all, bias_wide, s1s, s1r, rs, rr, sib, far_send, far_recv, fwd_send, fwd_recv,
+):
     spread = Spread(bias, bias_all, s1s, s1r, rs, rr)
     x, zl, y, col = spread.x, spread.zl, spread.y, spread.col
-    core = col % 2
-    z = (col // 2) * 4 + zl
-
-    def at_z(offset):
-        there = (z + offset + 8) % 8
-        return device(x, there % 4, y, (there // 4) * 2 + core)
-
-    def col_at(offset):
-        return (((z + offset + 8) % 8) // 4) * 2 + core
-
     sibling = device(x, zl, y, col ^ 1)
+    opposite = device(x, zl, y, col ^ 2)
     barrier = pltpu.get_barrier_semaphore()
     count = spread.greet(barrier)
-    for peer in (sibling, at_z(2), at_z(-2)):
+    for peer in (sibling, opposite):
         pl.semaphore_signal(barrier, inc=1, device_id=peer, device_id_type=MESH)
-    pl.semaphore_wait(barrier, count + 3)
-
-    def remote(src, dst, send, recv, to):
-        return pltpu.make_async_remote_copy(
-            src_ref=src, dst_ref=dst, send_sem=send, recv_sem=recv, device_id=to, device_id_type=MESH
+    pl.semaphore_wait(barrier, count + 2)
+
+    def far(r, block):
+        return remote(norm.at[r], norm_all.at[block, r], far_send.at[r], far_recv.at[r], opposite)
+
+    def forward(r, block):
+        return remote(
+            norm_all.at[col ^ 2, r], norm_all.at[block, r], fwd_send.at[r], fwd_recv.at[r], sibling
         )
 
-    def rows(way, c):
-        return pl.ds(8 * way + 2 * c, 2)
-
-    def step(way):
-        return 2 if way == 0 else -2
-
-    def hop1(way, c):
-        return remote(
-            norm.at[rows(way, c)], held.at[way, c], hop1s.at[way, c], hop1r.at[way, c], at_z(step(way))
-        )
-
-    def hop2(way, c):
-        return remote(
-            held.at[way, c],
-            norm_all.at[col_at(-step(way)), rows(way, c)],
-            hop2s.at[way, c],
-            hop2r.at[way, c],
-            at_z(step(way)),
-        )
-
-    def hop2_arrival(way, c):
-        return remote(
-            held.at[way, c],
-            norm_all.at[col ^ 2, rows(way, c)],
-            hop2s.at[way, c],
-            hop2r.at[way, c],
-            at_z(step(way)),
-        )
-
-    def forward(way, c, block):
-        return remote(
-            norm_all.at[col ^ 2, rows(way, c)],
-            norm_all.at[block, rows(way, c)],
-            fwds.at[way, c],
-            fwdr.at[way, c],
-            sibling,
-        )
+    def near(block):
+        return remote(norm, norm_all.at[block], sib.at[1], sib.at[2], sibling)
+
+    def pass_on(r):
+        far(r, col ^ 2).wait_recv()
+        forward(r, col ^ 2).start()
 
     spread.start()
-    for c in range(4):
-        for way in range(2):
-            hop1(way, c).start()
+    for r in range(16):
+        far(r, col).start()
     own = pltpu.make_async_copy(norm, norm_all.at[col], sib.at[0])
     own.start()
-    to_sibling = remote(norm, norm_all.at[col], sib.at[1], sib.at[2], sibling)
-    to_sibling.start()
+    near(col).start()
     spread.landed()
     spread.own()
-
-    def relay(way, c):
-        hop1(way, c).wait_recv()
-        hop2(way, c).start()
-
-    def last(way, c):
-        hop2_arrival(way, c).wait_recv()
-        forward(way, c, col ^ 2).start()
-
-    extra = []
-    for c in range(5):
-        for way in range(2):
-            if c < 4:
-                extra.append((relay, way, c))
-        for way in range(2):
-            if c > 0:
-                extra.append((last, way, c - 1))
     order = spread.order()
     for at, each in enumerate(order):
         spread.take(*each)
-        if at % 4 == 3 and extra:
-            fn, way, c = extra.pop(0)
-            fn(way, c)
-    for fn, way, c in extra:
-        fn(way, c)
+        if at % 6 == 5 and at // 6 < AHEAD:
+            pass_on(at // 6)
     own.wait()
-    to_sibling.wait_send()
-    remote(norm, norm_all.at[col ^ 1], sib.at[1], sib.at[2], sibling).wait_recv()
-    for c in range(4):
-        for way in range(2):
-            hop1(way, c).wait_send()
-            hop2(way, c).wait_send()
-            forward(way, c, col ^ 2).wait_send()
-            forward(way, c, col ^ 3).wait_recv()
+    near(col ^ 1).wait_recv()
+    for h in range(H):
+        for block in range(4):
+            masked = dead[:, pl.ds(256 * block, 256)]
+            for part in range(16):
+                some = bias_all[h // 2, block, part % 4, part // 4, h % 2].astype(F32)
+                bias_wide[h, pl.ds(16 * part, 16), pl.ds(256 * block, 256)] = some + masked
+    lane_head = lax.broadcasted_iota(jnp.int32, (256, CH), 1) // DH
+    ones = jnp.ones((1024, CH), BF16)
+
+    def attend(r, carry):
+        @pl.when(r < 16 - AHEAD)
+        def _():
+            pass_on(r + AHEAD)
+
+        forward(r, col ^ 3).wait_recv()
+        here = norm_all[:, r].reshape(4 * 256, CH)
+        kv = jnp.dot(here, att_in[:, CH : 3 * CH], preferred_element_type=F32).astype(BF16)
+        keys = kv[:, :CH]
+        values = jnp.concatenate([kv[:, CH:], ones], axis=1)
+        mine = norm[r]
+        queries = jnp.dot(mine, att_in[:, :CH], preferred_element_type=F32).astype(BF16)
+        gate = jax.nn.sigmoid(jnp.dot(mine, att_in[:, 3 * CH :], preferred_element_type=F32))
+        attended = jnp.zeros((256, CH), F32)
+        for h in range(H):
+            query = jnp.where(lane_head == h, queries, jnp.zeros((), BF16))
+            scores = lax.dot_general(
+                query, keys, (((1,), (1,)), ((), ())), preferred_element_type=F32
+            )
+            scores = scores * (1.0 / math.sqrt(DH)) + bias_wide[h]
+            top = jnp.max(scores, axis=-1, keepdims=True)
+            weights = jnp.exp(scores - top).astype(BF16)
+            summed = jnp.dot(weights, values, preferred_element_type=F32)
+            attended = jnp.where(lane_head == h, summed[:, :CH] / summed[:, CH:], attended)
+        attended = (attended * gate).astype(BF16)
+        add = jnp.dot(attended, att_out[...], preferred_element_type=F32)
+        new[r] = (mid[r].astype(F32) + add).astype(BF16)
+        return carry
+
+    lax.fori_loop(0, 16, attend, 0)
+    near(col).wait_send()
+    for r in range(16):
+        far(r, col).wait_send()
+        forward(r, col ^ 2).wait_send()
     spread.finish()
 
 
@@ -372,22 +366,28 @@
     )(right, left)
 
 
-def exchange_norms(bias, norm):
+VM = pl.BlockSpec(memory_space=pltpu.VMEM)
+
+
+def finish(bias, norm, mid, dead, att_in, att_out):
     return pl.pallas_call(
-        norm_exchange,
-        name="norm_exchange",
-        out_shape=(
-            jax.ShapeDtypeStruct((2, 4, 4, 4) + bias.shape[1:], bias.dtype),
-            jax.ShapeDtypeStruct((4,) + norm.shape, norm.dtype),
-        ),
-        in_specs=[ANY, ANY],
-        out_specs=(ANY, ANY),
-        scratch_shapes=[pltpu.VMEM((2, 4, 2) + norm.shape[1:], norm.dtype)]
+        finish_kernel,
+        name="finish",
+        out_shape=jax.ShapeDtypeStruct((16, 256, CH), BF16),
+        in_specs=[VM] * 6,
+        out_specs=VM,
+        scratch_shapes=[
+            pltpu.VMEM((2, 4, 4, 4) + bias.shape[1:], BF16),
+            pltpu.VMEM((4,) + norm.shape, BF16),
+            pltpu.VMEM((H, 256, 1024), F32),
+        ]
         + SPREAD_SEMS
         + [pltpu.SemaphoreType.DMA((3,))]
-        + [pltpu.SemaphoreType.DMA((2, 4))] * 6,
-        compiler_params=pltpu.CompilerParams(collective_id=1, has_side_effects=True),
-    )(bias, norm)
+        + [pltpu.SemaphoreType.DMA((16,))] * 4,
+        compiler_params=pltpu.CompilerParams(
+            collective_id=1, has_side_effects=True, vmem_limit_bytes=48 << 20
+        ),
+    )(bias, norm, mid, dead, att_in, att_out)
 
 
 def triangle_kernel(
@@ -476,70 +476,6 @@
     )
 
 
-TILE = 128
-
-
-def attention_kernel(own, norm, mid, bias, dead, att_in, att_out, new, bias_wide):
-    row = pl.program_id(0)
-
-    @pl.when(row == 0)
-    def _():
-        for h in range(H):
-            for block in range(4):
-                masked = dead[:, pl.ds(256 * block, 256)]
-                for part in range(16):
-                    some = bias[h // 2, block, part % 4, part // 4, h % 2].astype(F32)
-                    bias_wide[h, pl.ds(16 * part, 16), pl.ds(256 * block, 256)] = some + masked
-
-    here = norm[...].reshape(4 * 256, CH)
-    kv = jnp.dot(here, att_in[:, CH : 3 * CH], preferred_element_type=F32).astype(BF16)
-    keys = kv[:, :CH]
-    values = jnp.concatenate([kv[:, CH:], jnp.ones((1024, CH), BF16)], axis=1)
-    mine = own[0]
-    queries = jnp.dot(mine, att_in[:, :CH], preferred_element_type=F32).astype(BF16)
-    gate = jax.nn.sigmoid(jnp.dot(mine, att_in[:, 3 * CH :], preferred_element_type=F32))
-    lane_head = lax.broadcasted_iota(jnp.int32, (TILE, CH), 1) // DH
-    for t in range(256 // TILE):
-        rows = slice(t * TILE, (t + 1) * TILE)
-        attended = jnp.zeros((TILE, CH), F32)
-        for h in range(H):
-            query = jnp.where(lane_head == h, queries[rows], jnp.zeros((), BF16))
-            scores = lax.dot_general(
-                query, keys, (((1,), (1,)), ((), ())), preferred_element_type=F32
-            )
-            scores = scores * (1.0 / math.sqrt(DH)) + bias_wide[h, pl.ds(t * TILE, TILE), :]
-            top = jnp.max(scores, axis=-1, keepdims=True)
-            weights = jnp.exp(scores - top).astype(BF16)
-            summed = jnp.dot(weights, values, preferred_element_type=F32)
-            attended = jnp.where(lane_head == h, summed[:, :CH] / summed[:, CH:], attended)
-        attended = (attended * gate[rows]).astype(BF16)
-        add = jnp.dot(attended, att_out[...], preferred_element_type=F32)
-        new[0, pl.ds(t * TILE, TILE), :] = (mid[0, pl.ds(t * TILE, TILE), :].astype(F32) + add).astype(BF16)
-
-
-def attention(own, norm_all, mid, bias_all, dead, att_in, att_out):
-    whole = lambda *shape: pl.BlockSpec(shape, lambda t: (0,) * len(shape))
-    one_row = pl.BlockSpec((1, 256, CH), lambda t: (t, 0, 0))
-    return pl.pallas_call(
-        attention_kernel,
-        name="attention",
-        grid=(16,),
-        out_shape=jax.ShapeDtypeStruct((16, 256, CH), BF16),
-        in_specs=[
-            one_row,
-            pl.BlockSpec((4, 1, 256, CH), lambda t: (0, t, 0, 0)),
-            one_row,
-            whole(2, 4, 4, 4, 2, 16, 256),
-            whole(1, 1024),
-            whole(CH, 4 * CH),
-            whole(CH, CH),
-        ],
-        out_specs=one_row,
-        scratch_shapes=[pltpu.VMEM((H, 256, 1024), F32)],
-        compiler_params=pltpu.CompilerParams(vmem_limit_bytes=48 << 20),
-    )(own, norm_all, mid, bias_all, dead, att_in, att_out)
-
-
 def body(
     pair_rep, chain_len, tri_gain, tri_in, sum_gain, tri_out, att_gain, att_in, att_bias, att_out
 ):
@@ -561,9 +497,8 @@
     mid, norm, bias = triangle(
         right_all, left_all, pair_rep, tri_gain, tri_in, sum_gain, tri_out, att_gain, att_bias
     )
-    bias_all, norm_all = exchange_norms(bias, norm)
     dead = jnp.where(live_all > 0.5, 0.0, NEG_SCORE).reshape(1, -1)
-    return attention(norm, norm_all, mid, bias_all, dead, att_in, att_out)
+    return finish(bias, norm, mid, dead, att_in, att_out)
 
 
 def solution(mesh):

time: 206 us -> 194 us (0.942)
  Pallas kernels: 183 us -> 175 us
  local copies, waits for them, and re-layouts: 13.3 us -> 9.9 us
    pallas_call x2 -> x1, Pallas kernels: 112 us -> 104 us  [finish(): pl.pallas_call(finish_kernel, name='finish', out_shape=jax.ShapeDtypeStru...]
    unnamed x28 -> x23, local copies, waits for them, and re-layouts: 12.4 us -> 8.98 us
where the time goes in v2:
time: 194 us; the launch traced here: 190 us
  Pallas kernels  175 us (90%)
  local copies, waits for them, and re-layouts  9.9 us (5%)
  other arithmetic  4.66 us (2%)
    pallas_call x1, Pallas kernels, finish(): pl.pallas_call(finish_kernel, name='finish', out_shape=jax.ShapeDtypeStru...  104 us
    pallas_call x1, Pallas kernels, exchange_edges(): pl.pallas_call(edge_exchange, name='edge_exchange', out_shape=(jax.ShapeD...  48.7 us
    pallas_call x1, Pallas kernels, triangle(): pl.pallas_call(triangle_kernel, name='triangle', grid=(16,), out_shape=(j...  21.6 us
    unnamed x23, local copies, waits for them, and re-layouts  8.98 us

profile of v2, /device:TPU:25, one launch (start us, length us, event | category | flops | bytes accessed | tf_op | source)
XLA Modules:
  0.0 190.5 jit_solution(2043274448167745961)
XLA Ops:
  0.0 0.0 copy-start.10
  0.0 0.0 copy-start.4
  0.0 0.0 copy-start.6
  0.0 0.8 fusion.20
  0.8 0.1 reshape.128
  0.9 0.1 fusion.21
  1.0 0.1 broadcast_multiply_fusion
  1.0 0.9 convert_reduce_fusion
  2.0 1.0 fusion.2
  3.0 1.0 fusion.4
  4.0 1.1 fusion.15
  5.2 0.7 fusion.19
  5.9 48.7 %edge_exchange.1 = (bf16[2,4,4,4,8,16,128]{6,5,4,3,2,1,0:T(8,128)(2,1)}, bf16[4,16,16,128]{3,2,1,0:T(8,128)(2,1)}) custom-call(bf16[2,8,16,128]{3,2,1,0:T(8,128)(2,1)} %bitcast.15, bf16[16,16,128]{2,1,0:T(8,128)(2,1)} %get-tuple-element.27.left), custom_call_target="tpu_custom_call" | custom-call | tf_op jit(solution)/shard_map/edge_exchange/pallas_call | solution.py:350
  54.6 0.7 scatter.4.att_bias
  55.3 0.0 copy-start
  55.3 2.2 %copy-done = bf16[2,4,4,4,8,16,128]{6,5,4,3,2,1,0:T(8,128)(2,1)S(1)} copy-done((bf16[2,4,4,4,8,16,128]{6,5,4,3,2,1,0:T(8,128)(2,1)S(1)}, bf16[2,4,4,4,8,16,128]{6,5,4,3,2,1,0:T(8,128)(2,1)}, u32[]{:S(2)}) %copy-start) | copy-done | bytes 4194328
  57.5 1.2 copy-done.1
  58.7 0.0 copy-start.2
  58.7 0.9 copy-done.2
  59.7 0.9 copy-done.3
  60.6 0.8 copy-done.5
  61.4 0.7 copy-done.7
  62.0 0.7 copy-done.8
  62.7 0.7 copy-done.9
  63.3 21.6 %triangle.1 = (bf16[16,256,128]{2,1,0:T(8,128)(2,1)S(1)}, bf16[16,256,128]{2,1,0:T(8,128)(2,1)S(1)}, bf16[2,2,16,256]{3,2,1,0:T(8,128)(2,1)S(1)}) custom-call(bf16[2,4,4,4,8,16,128]{6,5,4,3,2,1,0:T(8,128)(2,1)S(1)} %copy-done, bf16[4,16,16,128]{3,2,1,0:T(8,128)(2,1)S(1)} %copy-done.3, bf16[16,256,128]{2,1,0:T(8,128)(2,1)S(1)} %copy-done.1, ...), custom_call_target="tpu_custom_call" | custom-call | tf_op jit(solution)/shard_map/triangle/pallas_call | solution.py:442
  84.9 0.0 copy-done.10
  84.9 0.1 compare_select_fusion
  85.0 0.1 select_n.23.dead
  85.1 0.0 copy-done.4
  85.1 0.0 copy-done.6
  85.1 104.4 %finish.1 = bf16[16,256,128]{2,1,0:T(8,128)(2,1)S(1)} custom-call(bf16[2,2,16,256]{3,2,1,0:T(8,128)(2,1)S(1)} %get-tuple-element.24.bias, bf16[16,256,128]{2,1,0:T(8,128)(2,1)S(1)} %get-tuple-element.25.norm, bf16[16,256,128]{2,1,0:T(8,128)(2,1)S(1)} %get-tuple-element.26.mid, f32[1,1024]{1,0:T(1,128)S(1)} %select_n.23.dead, bf16[128,512]{1,0:T(8,128)(2,1)S(1)} %copy-done.4, ...), custom_call_target="tpu_custom_call" | custom-call | tf_op jit(solution)/shard_map/finish/pallas_call | solution.py:373
  189.5 1.0 copy.20
  (8 shorter events, 0.0 us)
Async XLA Ops:
  0.0 84.9 %copy-start.10 = (s32[16]{0:T(128)S(1)}, s32[16]{0:T(128)}, u32[]{:S(2)}) copy-start(s32[16]{0:T(128)} %param.13) | copy-start | bytes 196
  0.0 85.1 %copy-start.4 = (bf16[128,512]{1,0:T(8,128)(2,1)S(1)}, bf16[128,512]{1,0:T(8,128)(2,1)}, u32[]{:S(2)}) copy-start(bf16[128,512]{1,0:T(8,128)(2,1)} %att_in.1) | copy-start | bytes 393220
  0.0 85.1 %copy-start.6 = (bf16[128,128]{1,0:T(8,128)(2,1)S(1)}, bf16[128,128]{1,0:T(8,128)(2,1)}, u32[]{:S(2)}) copy-start(bf16[128,128]{1,0:T(8,128)(2,1)} %att_out.1) | copy-start | bytes 98308
  55.3 2.2 %copy-start = (bf16[2,4,4,4,8,16,128]{6,5,4,3,2,1,0:T(8,128)(2,1)S(1)}, bf16[2,4,4,4,8,16,128]{6,5,4,3,2,1,0:T(8,128)(2,1)}, u32[]{:S(2)}) copy-start(bf16[2,4,4,4,8,16,128]{6,5,4,3,2,1,0:T(8,128)(2,1)} %get-tuple-element.22.right) | copy-start | bytes 12582916
  57.5 1.2 copy-start.1
  58.7 0.9 copy-start.2
  59.7 0.9 copy-start.3
  60.6 0.8 copy-start.5
  61.4 0.7 copy-start.7
  62.0 0.7 copy-start.8
  62.7 0.7 copy-start.9

commit v3 on v2

v3 whole, which is shorter than its diff:
```python
import math

import jax
import jax.numpy as jnp
from jax import lax
from jax.experimental import pallas as pl
from jax.experimental.pallas import tpu as pltpu
from jax.sharding import PartitionSpec as P

CH = 128
H = 4
DH = 32
KCD = 16
SLOT = 64
EPSILON = 1e-05
NEG_SCORE = -1e30
MESH = pl.DeviceIdType.MESH
F32 = jnp.float32
BF16 = jnp.bfloat16


def layer_norm(values, norm_gain):
    values = values.astype(F32)
    centre = values - jnp.mean(values, axis=-1, keepdims=True)
    spread = jnp.mean(centre * centre, axis=-1, keepdims=True)
    return centre * lax.rsqrt(spread + EPSILON) * norm_gain


def place():
    row = lax.axis_index("row")
    col = lax.axis_index("col")
    return row // 16, (row // 4) % 4, row % 4, col


def device(x, zl, y, col):
    return (x * 16 + zl * 4 + y, col)


class Spread:
    def __init__(self, pay, buf, s1_send, s1_recv, ring_send, ring_recv):
        self.pay, self.buf = pay, buf
        self.s1_send, self.s1_recv = s1_send, s1_recv
        self.ring_send, self.ring_recv = ring_send, ring_recv
        self.x, self.zl, self.y, self.col = place()
        self.swapped = self.x != self.col
        self.sent = []

    def partner(self):
        return device(self.col, self.zl, self.y, self.x)

    def line(self, i):
        return device(self.x, (self.zl + i) % 4, self.y, self.col)

    def neighbour(self, h, axis, d):
        along_y = (h == 0) == (axis == 0)
        if along_y:
            return device(self.x, self.zl, (self.y + d + 4) % 4, self.col)
        return device((self.x + d + 4) % 4, self.zl, self.y, self.col)

    def greet(self, barrier):
        def hello(to):
            pl.semaphore_signal(barrier, inc=1, device_id=to, device_id_type=MESH)

        for i in range(1, 4):
            hello(self.line(i))
        for axis in range(2):
            for d in (1, -1):
                hello(self.neighbour(0, axis, d))

        @pl.when(self.swapped)
        def _():
            hello(self.partner())

        return 7 + self.swapped.astype(jnp.int32)

    def swap(self, arrival):
        into = (self.x, self.zl) if arrival else (self.col, self.zl)
        return pltpu.make_async_remote_copy(
            src_ref=self.pay,
            dst_ref=self.buf.at[:, into[0], self.y, into[1]],
            send_sem=self.s1_send.at[0],
            recv_sem=self.s1_recv.at[0],
            device_id=self.partner(),
            device_id_type=MESH,
        )

    def keep(self):
        return pltpu.make_async_copy(
            self.pay, self.buf.at[:, self.x, self.y, self.zl], self.s1_send.at[0]
        )

    def share(self, i, arrival):
        block = self.buf.at[:, self.x, self.y, (self.zl + 4 - i) % 4 if arrival else self.zl]
        return pltpu.make_async_remote_copy(
            src_ref=block,
            dst_ref=block,
            send_sem=self.s1_send.at[i],
            recv_sem=self.s1_recv.at[i],
            device_id=self.line(i),
            device_id_type=MESH,
        )

    def start(self):
        @pl.when(self.swapped)
        def _():
            self.swap(False).start()

        @pl.when(jnp.logical_not(self.swapped))
        def _():
            self.keep().start()

    def landed(self):
        @pl.when(self.swapped)
        def _():
            self.swap(True).wait_recv()
            self.swap(False).wait_send()

        @pl.when(jnp.logical_not(self.swapped))
        def _():
            self.keep().wait()

        for i in (1, 3, 2):
            self.share(i, False).start()
        for i in (1, 3, 2):
            self.share(i, True).wait_recv()

    def piece(self, h, f, s, sub):
        xi, yi = (s, f) if h == 0 else (f, s)
        return self.buf.at[h, (self.x + xi) % 4, (self.y + yi) % 4, pl.ds(2 * sub, 2)]

    def slot(self, h, f, s, sub):
        return ((h * 4 + f) * 4 + s) * 2 + sub

    def send(self, h, f, s, sub, axis, d):
        there = ((f - d) % 4, s) if axis == 0 else (f, (s - d) % 4)
        copy = pltpu.make_async_remote_copy(
            src_ref=self.piece(h, f, s, sub),
            dst_ref=self.piece(h, f, s, sub),
            send_sem=self.ring_send.at[len(self.sent)],
            recv_sem=self.ring_recv.at[self.slot(h, *there, sub)],
            device_id=self.neighbour(h, axis, d),
            device_id_type=MESH,
        )
        copy.start()
        self.sent.append(copy)

    def own(self):
        for axis in range(2):
            for step in range(2):
                for h in range(2):
                    self.send(h, 0, 0, step, axis, 1)
                    self.send(h, 0, 0, 1 - step, axis, -1)

    def arrive(self, h, f, s, sub):
        pltpu.make_async_remote_copy(
            src_ref=self.piece(h, f, s, sub),
            dst_ref=self.piece(h, f, s, sub),
            send_sem=self.ring_send.at[0],
            recv_sem=self.ring_recv.at[self.slot(h, f, s, sub)],
            device_id=self.neighbour(h, 0, 1),
            device_id_type=MESH,
        ).wait_recv()

    def take(self, h, f, s, sub):
        self.arrive(h, f, s, sub)
        if s == 0:
            if f == 3 and sub == 0:
                self.send(h, f, s, sub, 0, 1)
            if f == 1 and sub == 1:
                self.send(h, f, s, sub, 0, -1)
            self.send(h, f, s, sub, 1, 1 if sub == 0 else -1)
            self.send(h, f, s, sub, 1, -1 if sub == 0 else 1)
        else:
            if s == 3 and sub == 0:
                self.send(h, f, s, sub, 1, 1)
            if s == 1 and sub == 1:
                self.send(h, f, s, sub, 1, -1)

    def order(self):
        near = [(3, 0), (1, 1), (3, 1), (1, 0)]
        steps = [(a, 0, sub) for a, sub in near]
        steps += [(0, a, sub) for a, sub in near]
        steps += [(2, 0, 0), (2, 0, 1)]
        for f in (3, 1):
            steps += [(f, a, sub) for a, sub in near]
        steps += [(0, 2, 0), (0, 2, 1)]
        steps += [(2, a, sub) for a, sub in near]
        steps += [(f, 2, sub) for f in (3, 1, 2) for sub in range(2)]
        return [(h, *step) for step in steps for h in range(2)]

    def finish(self):
        for i in range(1, 4):
            self.share(i, False).wait_send()
        for copy in self.sent:
            copy.wait_send()


SPREAD_SEMS = [
    pltpu.SemaphoreType.DMA((4,)),
    pltpu.SemaphoreType.DMA((4,)),
    pltpu.SemaphoreType.DMA((60,)),
    pltpu.SemaphoreType.DMA((64,)),
]


def remote(src, dst, send, recv, to):
    return pltpu.make_async_remote_copy(
        src_ref=src, dst_ref=dst, send_sem=send, recv_sem=recv, device_id=to, device_id_type=MESH
    )


AHEAD = 2


def sigmoid(v):
    return jax.nn.sigmoid(v)


def whole_kernel(
    chain_len, pair_hbm, tri_gain, tri_in, sum_gain, tri_out, att_gain, att_in, att_bias, att_out, new,
    pair, group, edges, left, right, right_all, left_all, left_wide, sums, gates, mid, norm,
    bias_rows, bias, bias_all, norm_all, bias_wide,
    a_s1s, a_s1r, a_rs, a_rr, left_send, left_recv, load,
    b_s1s, b_s1r, b_rs, b_rr, near_sem, far_send, far_recv, fwd_send, fwd_recv,
):
    first = Spread(right, right_all, a_s1s, a_s1r, a_rs, a_rr)
    second = Spread(bias, bias_all, b_s1s, b_s1r, b_rs, b_rr)
    x, zl, y, col = first.x, first.zl, first.y, first.col
    row = lax.axis_index("row")
    sibling = device(x, zl, y, col ^ 1)
    opposite = device(x, zl, y, col ^ 2)
    load_group = pltpu.make_async_copy(pair_hbm.at[:, pl.ds(0, KCD)], group, load.at[0])
    load_pair = pltpu.make_async_copy(pair_hbm, pair, load.at[1])
    load_group.start()
    load_pair.start()
    barrier = pltpu.get_barrier_semaphore()
    count = first.greet(barrier)
    for peer in (sibling, opposite):
        pl.semaphore_signal(barrier, inc=1, device_id=peer, device_id_type=MESH)

    load_group.wait()
    tri_norm = layer_norm(group[...].reshape(256, CH), tri_gain[...]).astype(BF16)
    proj = jnp.dot(tri_norm, tri_in[:, : 4 * CH], preferred_element_type=F32)
    cell = lax.broadcasted_iota(jnp.int32, (256, CH), 0)
    row_live = (row % 4) * 16 + cell // 16 < chain_len[row // 4]
    col_live = cell % 16 < chain_len[col * 4]
    live = jnp.where(row_live, 1.0, 0.0) * jnp.where(col_live, 1.0, 0.0)
    edges[0] = sigmoid(proj[:, :CH]) * proj[:, CH : 2 * CH] * live
    edges[1] = sigmoid(proj[:, 2 * CH : 3 * CH]) * proj[:, 3 * CH :] * live
    for k in range(16):
        left[k] = edges[0, pl.ds(k, 16, stride=16), :].astype(BF16)
        right[k // 8, k % 8] = edges[1, pl.ds(k, 16, stride=16), :].astype(BF16)

    pl.semaphore_wait(barrier, count + 2)
    first.start()
    left_near = remote(left, left_all.at[col], left_send.at[0], left_recv.at[0], sibling)
    left_far = remote(left, left_all.at[col], left_send.at[1], left_recv.at[1], opposite)
    left_near.start()
    left_far.start()
    load_pair.wait()

    def prepare(i, carry):
        normed = layer_norm(pair[i], tri_gain[...]).astype(BF16)
        gates[i] = sigmoid(jnp.dot(normed, tri_in[:, 4 * CH :], preferred_element_type=F32))
        sums[i] = jnp.zeros((16, 16, CH), F32)
        return carry

    lax.fori_loop(0, 16, prepare, 0)
    first.landed()
    first.own()

    def left_forward(block):
        return remote(
            left_all.at[col ^ 2], left_all.at[block], left_send.at[2], left_recv.at[2], sibling
        )

    remote(left, left_all.at[col ^ 2], left_send.at[1], left_recv.at[1], opposite).wait_recv()
    left_forward(col ^ 2).start()
    remote(left, left_all.at[col ^ 1], left_send.at[0], left_recv.at[0], sibling).wait_recv()
    left_wide[pl.ds(16 * col, 16)] = left[...].astype(F32)
    for j in (1, 2):
        left_wide[pl.ds(16 * (col ^ j), 16)] = left_all[col ^ j].astype(F32)
    left_forward(col ^ 3).wait_recv()
    left_wide[pl.ds(16 * (col ^ 3), 16)] = left_all[col ^ 3].astype(F32)

    def contract(h, f, s):
        xi, yi = (s, f) if h == 0 else (f, s)
        xi, yi = (x + xi) % 4, (y + yi) % 4

        def tile(z, carry):
            part = z * 4 + yi

            def tokens(q, total):
                total = list(total)
                for u in range(2):
                    k = 2 * q + u
                    edge = right_all[h, xi, yi, z, k].astype(F32)
                    for i in range(16):
                        total[i] = total[i] + edge * left_wide[xi * 16 + h * 8 + k, pl.ds(i, 1), :]
                return tuple(total)

            total = lax.fori_loop(0, 4, tokens, tuple(sums[i, part] for i in range(16)))
            for i in range(16):
                sums[i, part] = total[i]
            return carry

        lax.fori_loop(0, 4, tile, 0)

    contract(0, 0, 0)
    contract(1, 0, 0)
    seen = {}
    for h, f, s, sub in first.order():
        first.take(h, f, s, sub)
        seen[(h, f, s)] = seen.get((h, f, s), 0) + 1
        if seen[(h, f, s)] == 2:
            contract(h, f, s)
    first.finish()
    left_near.wait_send()
    left_far.wait_send()
    left_forward(col ^ 2).wait_send()

    def close(i, carry):
        sum_norm = layer_norm(sums[i].reshape(256, CH), sum_gain[...]).astype(BF16)
        update = jnp.dot(sum_norm, tri_out[...], preferred_element_type=F32)
        mid_row = (pair[i].astype(F32) + gates[i] * update).astype(BF16)
        mid[i] = mid_row
        att = layer_norm(mid_row, att_gain[...]).astype(BF16)
        norm[i] = att
        norm_all[col, i] = att
        rows = lax.dot_general(att_bias[...], att, (((1,), (1,)), ((), ())), preferred_element_type=F32)
        for h in range(H):
            bias_rows[h, pl.ds(i, 1), :] = rows[h : h + 1]
        return carry

    lax.fori_loop(0, 16, close, 0)
    for h in range(H):
        bias[h // 2, h % 2] = bias_rows[h].astype(BF16)
    second.start()

    def far(r, block):
        return remote(norm.at[r], norm_all.at[block, r], far_send.at[r], far_recv.at[r], opposite)

    def forward(r, block):
        return remote(
            norm_all.at[col ^ 2, r], norm_all.at[block, r], fwd_send.at[r], fwd_recv.at[r], sibling
        )

    def near(block):
        return remote(norm, norm_all.at[block], near_sem.at[0], near_sem.at[1], sibling)

    def pass_on(r):
        far(r, col ^ 2).wait_recv()
        forward(r, col ^ 2).start()

    near(col).start()
    second.landed()
    second.own()
    for r in range(16):
        far(r, col).start()
    for each in second.order():
        second.take(*each)
    for r in range(AHEAD):
        pass_on(r)
    near(col ^ 1).wait_recv()
    lane = lax.broadcasted_iota(jnp.int32, (16, 256), 1)
    for block in range(4):
        length = jnp.zeros((16, 256), jnp.int32)
        for c in range(4):
            length = jnp.where(lane // SLOT == c, chain_len[block * 4 + c], length)
        masked = jnp.where(lane % SLOT < length, 0.0, NEG_SCORE)
        for h in range(H):
            for part in range(16):
                some = bias_all[h // 2, block, part % 4, part // 4, h % 2].astype(F32)
                bias_wide[h, pl.ds(16 * part, 16), pl.ds(256 * block, 256)] = some + masked
    lane_head = lax.broadcasted_iota(jnp.int32, (256, CH), 1) // DH
    ones = jnp.ones((1024, CH), BF16)

    def attend(r, carry):
        @pl.when(r < 16 - AHEAD)
        def _():
            pass_on(r + AHEAD)

        forward(r, col ^ 3).wait_recv()
        here = norm_all[:, r].reshape(4 * 256, CH)
        kv = jnp.dot(here, att_in[:, CH : 3 * CH], preferred_element_type=F32).astype(BF16)
        keys = kv[:, :CH]
        values = jnp.concatenate([kv[:, CH:], ones], axis=1)
        mine = norm[r]
        queries = jnp.dot(mine, att_in[:, :CH], preferred_element_type=F32).astype(BF16)
        gate = jax.nn.sigmoid(jnp.dot(mine, att_in[:, 3 * CH :], preferred_element_type=F32))
        attended = jnp.zeros((256, CH), F32)
        for h in range(H):
            query = jnp.where(lane_head == h, queries, jnp.zeros((), BF16))
            scores = lax.dot_general(
                query, keys, (((1,), (1,)), ((), ())), preferred_element_type=F32
            )
            scores = scores * (1.0 / math.sqrt(DH)) + bias_wide[h]
            top = jnp.max(scores, axis=-1, keepdims=True)
            weights = jnp.exp(scores - top).astype(BF16)
            summed = jnp.dot(weights, values, preferred_element_type=F32)
            attended = jnp.where(lane_head == h, summed[:, :CH] / summed[:, CH:], attended)
        attended = (attended * gate).astype(BF16)
        add = jnp.dot(attended, att_out[...], preferred_element_type=F32)
        new[r] = (mid[r].astype(F32) + add).astype(BF16)
        return carry

    lax.fori_loop(0, 16, attend, 0)
    near(col).wait_send()
    for r in range(16):
        far(r, col).wait_send()
        forward(r, col ^ 2).wait_send()
    second.finish()


ANY = pl.BlockSpec(memory_space=pl.ANY)
VM = pl.BlockSpec(memory_space=pltpu.VMEM)
SM = pl.BlockSpec(memory_space=pltpu.SMEM)


def body(
    pair_rep, chain_len, tri_gain, tri_in, sum_gain, tri_out, att_gain, att_in, att_bias, att_out
):
    bias_rows = jnp.pad(att_bias.T, ((0, 8 - H), (0, 0)))
    vmem = pltpu.VMEM
    return pl.pallas_call(
        whole_kernel,
        name="whole",
        out_shape=jax.ShapeDtypeStruct((16, 256, CH), BF16),
        in_specs=[SM, ANY] + [VM] * 8,
        out_specs=VM,
        scratch_shapes=[
            vmem((16, 256, CH), BF16),
            vmem((16, KCD, CH), BF16),
            vmem((2, 256, CH), F32),
            vmem((16, 16, CH), BF16),
            vmem((2, 8, 16, CH), BF16),
            vmem((2, 4, 4, 4, 8, 16, CH), BF16),
            vmem((4, 16, 16, CH), BF16),
            vmem((64, 16, CH), F32),
            vmem((16, 16, 16, CH), F32),
            vmem((16, 256, CH), F32),
            vmem((16, 256, CH), BF16),
            vmem((16, 256, CH), BF16),
            vmem((H, 16, 256), F32),
            vmem((2, 2, 16, 256), BF16),
            vmem((2, 4, 4, 4, 2, 16, 256), BF16),
            vmem((4, 16, 256, CH), BF16),
            vmem((H, 256, 1024), F32),
        ]
        + SPREAD_SEMS
        + [pltpu.SemaphoreType.DMA((3,)), pltpu.SemaphoreType.DMA((3,)), pltpu.SemaphoreType.DMA((2,))]
        + SPREAD_SEMS
        + [pltpu.SemaphoreType.DMA((2,))]
        + [pltpu.SemaphoreType.DMA((16,))] * 4,
        compiler_params=pltpu.CompilerParams(
            collective_id=0, has_side_effects=True, vmem_limit_bytes=56 << 20
        ),
    )(
        chain_len, pair_rep, tri_gain.reshape(1, CH), tri_in, sum_gain.reshape(1, CH), tri_out,
        att_gain.reshape(1, CH), att_in, bias_rows, att_out,
    )


def solution(mesh):
    placed = (P("row", "col", None), P(), P(), P(), P(), P(), P(), P(), P(), P())
    return jax.shard_map(
        body, mesh=mesh, in_specs=placed, out_specs=P("row", "col", None), check_vma=False
    )
```

time: 194 us -> 165 us (0.85)
  the two profiles are of different devices: /device:TPU:25 before, /device:TPU:129 now
where the time goes in v3:
time: 165 us
  Pallas kernels  162 us (98%)
  local copies, waits for them, and re-layouts  3.56 us (2%)
    pallas_call x1, Pallas kernels, body(): pl.pallas_call(whole_kernel, name='whole', out_shape=jax.ShapeDtypeStruct...  162 us

profile of v3, /device:TPU:129, one launch (start us, length us, event | category | flops | bytes accessed | tf_op | source)
XLA Modules:
  0.0 165.3 jit_solution(1846017510393392095)
XLA Ops:
  0.0 0.0 copy-start
  0.0 0.7 copy-done
  0.7 0.6 pad.4.att_bias
  1.3 161.7 %whole.1 = bf16[16,256,128]{2,1,0:T(8,128)(2,1)} custom-call(s32[16]{0:T(128)} %chain_len.1, bf16[16,256,128]{2,1,0:T(8,128)(2,1)} %pair_hbm.1, f32[1,128]{1,0:T(1,128)} %bitcast.5, bf16[128,640]{1,0:T(8,128)(2,1)} %tri_in.1, f32[1,128]{1,0:T(1,128)} %bitcast.6, bf16[128,128]{1,0:T(8,128)(2,1)} %tri_out.1, f32[1,128]{1,0:T(1,128)} %bitcast.7, ...), custom_call_target="tpu_custom_call" | custom-call | tf_op jit(solution)/shard_map/whole/pallas_call | solution.py:425
  163.0 2.3 %copy.12 = bf16[16,256,128]{2,1,0:T(8,128)(2,1)} copy(bf16[16,256,128]{2,1,0:T(8,128)(2,1)} %whole.1) | data formatting | bytes 2097152
Async XLA Ops:
  0.0 0.7 copy-start

commit v4 on v3

--- a/solution.py
+++ b/solution.py
@@ -210,6 +210,8 @@
 
 
 AHEAD = 2
+EARLY = 4
+FAR_AT = 4
 
 
 def sigmoid(v):
@@ -319,7 +321,10 @@
     left_far.wait_send()
     left_forward(col ^ 2).wait_send()
 
-    def close(i, carry):
+    def far(r, block):
+        return remote(norm.at[r], norm_all.at[block, r], far_send.at[r], far_recv.at[r], opposite)
+
+    def close_row(i):
         sum_norm = layer_norm(sums[i].reshape(256, CH), sum_gain[...]).astype(BF16)
         update = jnp.dot(sum_norm, tri_out[...], preferred_element_type=F32)
         mid_row = (pair[i].astype(F32) + gates[i] * update).astype(BF16)
@@ -330,16 +335,23 @@
         rows = lax.dot_general(att_bias[...], att, (((1,), (1,)), ((), ())), preferred_element_type=F32)
         for h in range(H):
             bias_rows[h, pl.ds(i, 1), :] = rows[h : h + 1]
+
+    def close(i, carry):
+        close_row(2 * i)
+        close_row(2 * i + 1)
+
+        @pl.when(i < EARLY // 2)
+        def _():
+            far(2 * i, col).start()
+            far(2 * i + 1, col).start()
+
         return carry
 
-    lax.fori_loop(0, 16, close, 0)
+    lax.fori_loop(0, 8, close, 0)
     for h in range(H):
         bias[h // 2, h % 2] = bias_rows[h].astype(BF16)
     second.start()
 
-    def far(r, block):
-        return remote(norm.at[r], norm_all.at[block, r], far_send.at[r], far_recv.at[r], opposite)
-
     def forward(r, block):
         return remote(
             norm_all.at[col ^ 2, r], norm_all.at[block, r], fwd_send.at[r], fwd_recv.at[r], sibling
@@ -355,10 +367,17 @@
     near(col).start()
     second.landed()
     second.own()
-    for r in range(16):
-        far(r, col).start()
-    for each in second.order():
+
+    def far_rest():
+        for r in range(EARLY, 16):
+            far(r, col).start()
+
+    z_here = (col // 2) * 4 + zl
+    pl.when(z_here == 0)(far_rest)
+    for at, each in enumerate(second.order()):
         second.take(*each)
+        if at == FAR_AT:
+            pl.when(z_here != 0)(far_rest)
     for r in range(AHEAD):
         pass_on(r)
     near(col ^ 1).wait_recv()
@@ -375,12 +394,7 @@
     lane_head = lax.broadcasted_iota(jnp.int32, (256, CH), 1) // DH
     ones = jnp.ones((1024, CH), BF16)
 
-    def attend(r, carry):
-        @pl.when(r < 16 - AHEAD)
-        def _():
-            pass_on(r + AHEAD)
-
-        forward(r, col ^ 3).wait_recv()
+    def attend_row(r):
         here = norm_all[:, r].reshape(4 * 256, CH)
         kv = jnp.dot(here, att_in[:, CH : 3 * CH], preferred_element_type=F32).astype(BF16)
         keys = kv[:, :CH]
@@ -402,9 +416,20 @@
         attended = (attended * gate).astype(BF16)
         add = jnp.dot(attended, att_out[...], preferred_element_type=F32)
         new[r] = (mid[r].astype(F32) + add).astype(BF16)
+
+    def attend(q, carry):
+        @pl.when(q < 7)
+        def _():
+            pass_on(2 * q + 2)
+            pass_on(2 * q + 3)
+
+        forward(2 * q, col ^ 3).wait_recv()
+        forward(2 * q + 1, col ^ 3).wait_recv()
+        attend_row(2 * q)
+        attend_row(2 * q + 1)
         return carry
 
-    lax.fori_loop(0, 16, attend, 0)
+    lax.fori_loop(0, 8, attend, 0)
     near(col).wait_send()
     for r in range(16):
         far(r, col).wait_send()

time: 165 us -> 133 us (0.81)
  the two profiles are of different devices: /device:TPU:129 before, /device:TPU:25 now
where the time goes in v4:
time: 133 us; the launch traced here: 131 us
  Pallas kernels  128 us (96%)
  local copies, waits for them, and re-layouts  3.56 us (3%)
    pallas_call x1, Pallas kernels, body(): pl.pallas_call(whole_kernel, name='whole', out_shape=jax.ShapeDtypeStruct...  128 us
    unnamed x3, local copies, waits for them, and re-layouts  2.97 us

profile of v4, /device:TPU:25, one launch (start us, length us, event | category | flops | bytes accessed | tf_op | source)
XLA Modules:
  0.0 131.1 jit_solution(12404853928312796729)
XLA Ops:
  0.0 0.0 copy-start
  0.0 0.7 copy-done
  0.7 0.6 pad.4.att_bias
  1.3 127.5 %whole.1 = bf16[16,256,128]{2,1,0:T(8,128)(2,1)} custom-call(s32[16]{0:T(128)} %chain_len.1, bf16[16,256,128]{2,1,0:T(8,128)(2,1)} %pair_hbm.1, f32[1,128]{1,0:T(1,128)} %bitcast.5, bf16[128,640]{1,0:T(8,128)(2,1)} %tri_in.1, f32[1,128]{1,0:T(1,128)} %bitcast.6, bf16[128,128]{1,0:T(8,128)(2,1)} %tri_out.1, f32[1,128]{1,0:T(1,128)} %bitcast.7, ...), custom_call_target="tpu_custom_call" | custom-call | tf_op jit(solution)/shard_map/whole/pallas_call | solution.py:450
  128.8 2.3 %copy.12 = bf16[16,256,128]{2,1,0:T(8,128)(2,1)} copy(bf16[16,256,128]{2,1,0:T(8,128)(2,1)} %whole.1) | data formatting | bytes 2097152
Async XLA Ops:
  0.0 0.7 copy-start

commit v5 on v4

--- a/solution.py
+++ b/solution.py
@@ -109,7 +109,7 @@
         def _():
             self.keep().start()
 
-    def landed(self):
+    def landed(self, during=None):
         @pl.when(self.swapped)
         def _():
             self.swap(True).wait_recv()
@@ -121,6 +121,8 @@
 
         for i in (1, 3, 2):
             self.share(i, False).start()
+        if during is not None:
+            during()
         for i in (1, 3, 2):
             self.share(i, True).wait_recv()
 
@@ -267,8 +269,8 @@
         sums[i] = jnp.zeros((16, 16, CH), F32)
         return carry
 
-    lax.fori_loop(0, 16, prepare, 0)
-    first.landed()
+    lax.fori_loop(0, 6, prepare, 0)
+    first.landed(lambda: lax.fori_loop(6, 16, prepare, 0))
     first.own()
 
     def left_forward(block):
@@ -373,11 +375,14 @@
             far(r, col).start()
 
     z_here = (col // 2) * 4 + zl
+    edge = (zl == 3) | (z_here == 4)
     pl.when(z_here == 0)(far_rest)
     for at, each in enumerate(second.order()):
         second.take(*each)
         if at == FAR_AT:
-            pl.when(z_here != 0)(far_rest)
+            pl.when((z_here != 0) & jnp.logical_not(edge))(far_rest)
+        if at == 9:
+            pl.when(edge)(far_rest)
     for r in range(AHEAD):
         pass_on(r)
     near(col ^ 1).wait_recv()
@@ -445,7 +450,6 @@
 def body(
     pair_rep, chain_len, tri_gain, tri_in, sum_gain, tri_out, att_gain, att_in, att_bias, att_out
 ):
-    bias_rows = jnp.pad(att_bias.T, ((0, 8 - H), (0, 0)))
     vmem = pltpu.VMEM
     return pl.pallas_call(
         whole_kernel,
@@ -482,7 +486,7 @@
         ),
     )(
         chain_len, pair_rep, tri_gain.reshape(1, CH), tri_in, sum_gain.reshape(1, CH), tri_out,
-        att_gain.reshape(1, CH), att_in, bias_rows, att_out,
+        att_gain.reshape(1, CH), att_in, att_bias.T, att_out,
     )
 
 

time: 133 us -> 130 us (0.977)
  Pallas kernels: 128 us -> 126 us
    unnamed x3 -> x1, local copies, waits for them, and re-layouts: 2.97 us -> 2.3 us
where the time goes in v5:
time: 130 us; the launch traced here: 129 us
  Pallas kernels  126 us (97%)
  local copies, waits for them, and re-layouts  2.3 us (2%)
    pallas_call x1, Pallas kernels, body(): pl.pallas_call(whole_kernel, name='whole', out_shape=jax.ShapeDtypeStruct...  126 us

profile of v5, /device:TPU:25, one launch (start us, length us, event | category | flops | bytes accessed | tf_op | source)
XLA Modules:
  0.0 128.8 jit_solution(3464907630510893819)
XLA Ops:
  0.0 126.5 %whole.1 = bf16[16,256,128]{2,1,0:T(8,128)(2,1)} custom-call(s32[16]{0:T(128)} %chain_len.1, bf16[16,256,128]{2,1,0:T(8,128)(2,1)} %pair_hbm.1, f32[1,128]{1,0:T(1,128)} %bitcast.5, bf16[128,640]{1,0:T(8,128)(2,1)} %tri_in.1, f32[1,128]{1,0:T(1,128)} %bitcast.6, bf16[128,128]{1,0:T(8,128)(2,1)} %tri_out.1, f32[1,128]{1,0:T(1,128)} %bitcast.7, ...), custom_call_target="tpu_custom_call" | custom-call | tf_op jit(solution)/shard_map/whole/pallas_call | solution.py:454
  126.5 2.3 %copy.12 = bf16[16,256,128]{2,1,0:T(8,128)(2,1)} copy(bf16[16,256,128]{2,1,0:T(8,128)(2,1)} %whole.1) | data formatting | bytes 2097152

commit v6 on v5

--- a/solution.py
+++ b/solution.py
@@ -318,10 +318,6 @@
         seen[(h, f, s)] = seen.get((h, f, s), 0) + 1
         if seen[(h, f, s)] == 2:
             contract(h, f, s)
-    first.finish()
-    left_near.wait_send()
-    left_far.wait_send()
-    left_forward(col ^ 2).wait_send()
 
     def far(r, block):
         return remote(norm.at[r], norm_all.at[block, r], far_send.at[r], far_recv.at[r], opposite)
@@ -440,6 +436,10 @@
         far(r, col).wait_send()
         forward(r, col ^ 2).wait_send()
     second.finish()
+    first.finish()
+    left_near.wait_send()
+    left_far.wait_send()
+    left_forward(col ^ 2).wait_send()
 
 
 ANY = pl.BlockSpec(memory_space=pl.ANY)

time: 130 us -> 130 us (level)
  no operation moved by 1% of the time
where the time goes in v6:
time: 130 us; the launch traced here: 129 us
  Pallas kernels  127 us (98%)
  local copies, waits for them, and re-layouts  2.3 us (2%)
    pallas_call x1, Pallas kernels, body(): pl.pallas_call(whole_kernel, name='whole', out_shape=jax.ShapeDtypeStruct...  127 us

profile of v6, /device:TPU:25, one launch (start us, length us, event | category | flops | bytes accessed | tf_op | source)
XLA Modules:
  0.0 128.8 jit_solution(1475935845211541306)
XLA Ops:
  0.0 126.5 %whole.1 = bf16[16,256,128]{2,1,0:T(8,128)(2,1)} custom-call(s32[16]{0:T(128)} %chain_len.1, bf16[16,256,128]{2,1,0:T(8,128)(2,1)} %pair_hbm.1, f32[1,128]{1,0:T(1,128)} %bitcast.5, bf16[128,640]{1,0:T(8,128)(2,1)} %tri_in.1, f32[1,128]{1,0:T(1,128)} %bitcast.6, bf16[128,128]{1,0:T(8,128)(2,1)} %tri_out.1, f32[1,128]{1,0:T(1,128)} %bitcast.7, ...), custom_call_target="tpu_custom_call" | custom-call | tf_op jit(solution)/shard_map/whole/pallas_call | solution.py:454
  126.5 2.3 %copy.12 = bf16[16,256,128]{2,1,0:T(8,128)(2,1)} copy(bf16[16,256,128]{2,1,0:T(8,128)(2,1)} %whole.1) | data formatting | bytes 2097152
